TPU v7x, 32 devices: a whole 2x2x4 slice. The times are simulated.
32 devices in a mesh: groups: 2 (over y), expert: 4 (over z), dp: 2 (over x), mp: 2 (over core).
Axes of the slice: x: 2, y: 2, z: 4, core: 2. Of those that a mesh axis runs over, the one named last changes fastest.
Arguments:
- latent: float32 [512, 2048], P(('groups', 'expert', 'dp', 'mp')), parts along dimension 0, may hold values from -6 to 6
- time_embedding: float32 [2048], replicated, may hold values from -6 to 6
- norm_gain: float32 [2, 2048], replicated, may hold values from 0.1 to 1.9
- router: float32 [2, 2048, 16], replicated, may hold values from -0.03125 to 0.03125
- up_proj: bfloat16 [2, 16, 2048, 1408], P(None, 'expert', None, 'dp'), may hold values from -0.125 to 0.125
- down_proj: bfloat16 [2, 16, 1408, 2048], P(None, 'expert', 'dp'), may hold values from -0.15625 to 0.15625
- routes: int32 [2, 2, 512, 2], P(None, None, ('groups', 'expert', 'dp', 'mp')), parts along dimension 2, may hold values from 0 to 15, all different within a row; in each aligned block of 16 rows (0 to 15, 16 to 31, ..., all dimensions but the last counted through in order) at most 2 rows name the same one
Outputs:
- next_latent: float32 [512, 2048], P(('groups', 'expert', 'dp', 'mp')), parts along dimension 0
- mean_velocity: float32 [512, 2048], P(('groups', 'expert', 'dp', 'mp')), parts along dimension 0
There are 2 independent parts, one for each index of `groups`. A program takes and returns all parts, laid end to end along the dimension named above; an argument that names none is the same for every part. Nothing has to cross between parts.
Inputs may be any that keep to these rules, and one draw needn't show every extreme that they name: `routes`: in each evaluation and layer, the 16 tokens of one device (aligned blocks along the token dimension) name any one expert at most 2 times, a bound that some block reaches by one device's tokens; a token's two experts differ.
All inputs are finite; a program needn't handle non-finite values.
Results may differ from a plain program's by a relative error of at most 0.0055.
Values may be sent and summed in bfloat16 or wider, within the bound.
No kernel may reach another device: no remote copies, remote signals or barrier semaphores. Data moves between devices by JAX's collectives and lax.ppermute only.
A program may use at most 128 MiB of HBM per device.

v0:
```python
import jax
import jax.numpy as jnp
from jax import lax
from jax.sharding import PartitionSpec as P

CAP = 2


epsilon = 1e-06
start_time = 1.0
step_size = -0.5


def local_block(state, gain, router_layer, up_layer, down_layer, chosen):
    tok_count = state.shape[0]
    model_width = state.shape[1]
    top_count = chosen.shape[1]
    experts = router_layer.shape[1]
    local_experts = up_layer.shape[0]
    inverse = lax.rsqrt(jnp.mean(state * state, axis=1, keepdims=True) + epsilon)
    scaled = state * inverse * gain[None, :]
    normed = scaled.astype(jnp.bfloat16)
    logits = jnp.dot(scaled, router_layer, precision=lax.Precision.HIGHEST)
    picked = jnp.take_along_axis(logits, chosen, axis=1)
    leading = jax.nn.sigmoid(picked[:, 0] - picked[:, 1])
    weights = jnp.stack([leading, 1.0 - leading], axis=1)
    flat_choice = chosen.reshape(-1)
    onehot = (flat_choice[:, None] == jnp.arange(experts, dtype=jnp.int32)[None, :]).astype(
        jnp.int32
    )
    before = jnp.cumsum(onehot, axis=0) - onehot
    position = jnp.sum(before * onehot, axis=1)
    slot_id = flat_choice * CAP + position
    targets = slot_id.reshape(tok_count, top_count)
    select = jnp.any(
        jnp.arange(experts * CAP, dtype=jnp.int32)[:, None, None] == targets[None, :, :], axis=2
    ).astype(jnp.bfloat16)
    buffer = (
        jnp.dot(select, normed, preferred_element_type=jnp.float32)
        .astype(jnp.bfloat16)
        .reshape(experts, CAP, model_width)
    )
    landed = lax.all_to_all(buffer, "expert", split_axis=0, concat_axis=0, tiled=True)
    arrived = lax.all_gather(landed[None], "dp", axis=0, tiled=True)
    group_count = arrived.shape[0]
    source_count = arrived.shape[1] // local_experts
    grouped = (
        arrived.reshape(group_count, source_count, local_experts, CAP, model_width)
        .transpose(2, 0, 1, 3, 4)
        .reshape(local_experts, group_count * source_count * CAP, model_width)
    )
    hidden = jax.nn.gelu(
        jnp.einsum("erd,edf->erf", grouped, up_layer, preferred_element_type=jnp.float32),
        approximate=True,
    ).astype(jnp.bfloat16)
    partial_value = jnp.einsum(
        "erf,efd->erd", hidden, down_layer, preferred_element_type=jnp.float32
    ).astype(jnp.bfloat16)
    partial_value = (
        partial_value.reshape(local_experts, group_count, source_count, CAP, model_width)
        .transpose(1, 2, 0, 3, 4)
        .reshape(group_count, source_count * local_experts, CAP, model_width)
    )
    owned = lax.all_to_all(partial_value, "dp", split_axis=0, concat_axis=0, tiled=True)
    summed = jnp.sum(owned.astype(jnp.float32), axis=0).astype(jnp.bfloat16)
    returned = lax.all_to_all(summed, "expert", split_axis=0, concat_axis=0, tiled=True)
    gathered = returned.reshape(experts * CAP, model_width)[slot_id].reshape(
        tok_count, top_count, model_width
    )
    return state + jnp.sum(weights[:, :, None] * gathered.astype(jnp.float32), axis=1)


def velocity(
    latent_now, time_now, section_routes, time_embedding, norm_gain, router, up_proj, down_proj
):
    state = latent_now + time_now * time_embedding[None, :]
    for layer_index in range(norm_gain.shape[0]):
        state = local_block(
            state,
            norm_gain[layer_index],
            router[layer_index],
            up_proj[layer_index],
            down_proj[layer_index],
            section_routes[layer_index],
        )
    return state - latent_now


def per_device(latent, time_embedding, norm_gain, router, up_proj, down_proj, routes):
    first = velocity(
        latent, start_time, routes[0], time_embedding, norm_gain, router, up_proj, down_proj
    )
    moved = latent + step_size * first
    second = velocity(
        moved,
        start_time + step_size,
        routes[1],
        time_embedding,
        norm_gain,
        router,
        up_proj,
        down_proj,
    )
    mean_velocity = 0.5 * (first + second)
    return (latent + step_size * mean_velocity, mean_velocity)


def solution(mesh):
    placed = (
        P(("groups", "expert", "dp", "mp"), None),
        P(),
        P(),
        P(),
        P(None, "expert", None, "dp"),
        P(None, "expert", "dp", None),
        P(None, None, ("groups", "expert", "dp", "mp"), None),
    )
    return jax.shard_map(
        per_device,
        mesh=mesh,
        in_specs=placed,
        out_specs=(
            P(("groups", "expert", "dp", "mp"), None),
            P(("groups", "expert", "dp", "mp"), None),
        ),
        check_vma=False,
    )
```

profile of v0, /device:TPU:0, one launch (start us, length us, event | category | flops | bytes accessed | tf_op | source)
XLA Modules:
  0.0 211.1 jit_solution(11158140217822368386)
XLA Ops:
  8.7 6.3 %all-to-all-start = ((bf16[16,2,2048]{2,1,0:T(2,128)(2,1)}), bf16[16,2,2048]{2,1,0:T(2,128)(2,1)S(1)}, u32[]{:S(2)}, u32[]{:S(2)}) async-start(bf16[16,2,2048]{2,1,0:T(2,128)(2,1)} %reshape.307), calls=%async_computation | async-start | bytes 262144 | tf_op jit(solution)/shard_map/all_to_all | solution.py:43
  21.2 5.6 %all-gather = bf16[32,2,2048]{2,1,0:T(2,128)(2,1)S(1)} all-gather(bf16[16,2,2048]{2,1,0:T(2,128)(2,1)S(1)} %all-to-all-done), channel_id=2, replica_groups=mesh['groups'=2,'expert'=4,'dp'=2,'mp'=2] {'dp'}, dimensions={0}, use_global_device_ids=true | all-gather | bytes 393216 | tf_op jit(solution)/shard_map/all_gather | solution.py:44
  27.1 6.0 %fusion.45 = bf16[4,16,704]{2,1,0:T(8,128)(2,1)S(1)} fusion(bf16[4,16,2048]{2,1,0:T(8,128)(2,1)S(1)} %reshape.309, bf16[2,4,2048,704]{2,3,1,0:T(8,128)(2,1)} %param.13), kind=kOutput, calls=%fused_computation.59 | convolution fusion | flops 184954880 | bytes 11886592 | tf_op jit(solution)/shard_map/erd,edf->erf/dot_general | solution.py:53
  33.1 5.9 %fusion.24 = bf16[4,16,2048]{2,1,0:T(8,128)(2,1)S(1)} fusion(bf16[4,16,704]{2,1,0:T(8,128)(2,1)S(1)} %fusion.45, bf16[2,4,704,2048]{3,2,1,0:T(8,128)(2,1)} %param.14), kind=kOutput, calls=%fused_computation.32 | convolution fusion | flops 184680448 | bytes 11886592 | tf_op jit(solution)/shard_map/erf,efd->erd/dot_general | solution.py:56
  40.1 3.4 %all-to-all-start.1 = ((bf16[2,16,2,2048]{3,2,1,0:T(2,128)(2,1)}), bf16[2,16,2,2048]{3,2,1,0:T(2,128)(2,1)S(1)}, u32[]{:S(2)}, u32[]{:S(2)}) async-start(bf16[2,16,2,2048]{3,2,1,0:T(2,128)(2,1)} %bitcast.9), calls=%async_computation.1 | async-start | bytes 524288 | tf_op jit(solution)/shard_map/all_to_all | solution.py:64
  44.3 4.4 %all-to-all-done.1 = bf16[2,16,2,2048]{3,2,1,0:T(2,128)(2,1)S(1)} async-done(((bf16[2,16,2,2048]{3,2,1,0:T(2,128)(2,1)}), bf16[2,16,2,2048]{3,2,1,0:T(2,128)(2,1)S(1)}, u32[]{:S(2)}, u32[]{:S(2)}) %all-to-all-start.1) | async-done | bytes 262176 | tf_op jit(solution)/shard_map/all_to_all | solution.py:64
  49.9 3.7 %all-to-all-start.2 = ((bf16[16,2,2048]{2,1,0:T(2,128)(2,1)}), bf16[16,2,2048]{2,1,0:T(2,128)(2,1)S(1)}, u32[]{:S(2)}, u32[]{:S(2)}) async-start(bf16[16,2,2048]{2,1,0:T(2,128)(2,1)} %reduce_sum.175), calls=%async_computation.2 | async-start | bytes 262144 | tf_op jit(solution)/shard_map/all_to_all | solution.py:66
  53.6 5.9 %all-to-all-done.2 = bf16[16,2,2048]{2,1,0:T(2,128)(2,1)S(1)} async-done(((bf16[16,2,2048]{2,1,0:T(2,128)(2,1)}), bf16[16,2,2048]{2,1,0:T(2,128)(2,1)S(1)}, u32[]{:S(2)}, u32[]{:S(2)}) %all-to-all-start.2) | async-done | bytes 131104 | tf_op jit(solution)/shard_map/all_to_all | solution.py:66
  62.0 3.3 %all-to-all-start.3 = ((bf16[16,2,2048]{2,1,0:T(2,128)(2,1)}), bf16[16,2,2048]{2,1,0:T(2,128)(2,1)S(1)}, u32[]{:S(2)}, u32[]{:S(2)}) async-start(bf16[16,2,2048]{2,1,0:T(2,128)(2,1)} %reshape.313), calls=%async_computation.3 | async-start | bytes 262144 | tf_op jit(solution)/shard_map/all_to_all | solution.py:43
  66.6 4.6 %all-to-all-done.3 = bf16[16,2,2048]{2,1,0:T(2,128)(2,1)S(1)} async-done(((bf16[16,2,2048]{2,1,0:T(2,128)(2,1)}), bf16[16,2,2048]{2,1,0:T(2,128)(2,1)S(1)}, u32[]{:S(2)}, u32[]{:S(2)}) %all-to-all-start.3) | async-done | bytes 131104 | tf_op jit(solution)/shard_map/all_to_all | solution.py:43
  71.2 5.6 %all-gather.1 = bf16[32,2,2048]{2,1,0:T(2,128)(2,1)S(1)} all-gather(bf16[16,2,2048]{2,1,0:T(2,128)(2,1)S(1)} %all-to-all-done.3), channel_id=3, replica_groups=mesh['groups'=2,'expert'=4,'dp'=2,'mp'=2] {'dp'}, dimensions={0}, use_global_device_ids=true | all-gather | bytes 393216 | tf_op jit(solution)/shard_map/all_gather | solution.py:44
  77.1 6.0 %fusion.57 = bf16[4,16,704]{2,1,0:T(8,128)(2,1)S(1)} fusion(bf16[4,16,2048]{2,1,0:T(8,128)(2,1)S(1)} %reshape.315, bf16[2,4,2048,704]{2,3,1,0:T(8,128)(2,1)} %param.13), kind=kOutput, calls=%fused_computation.67 | convolution fusion | flops 184954880 | bytes 11886592 | tf_op jit(solution)/shard_map/erd,edf->erf/dot_general | solution.py:53
  83.2 5.9 %fusion.30 = bf16[4,16,2048]{2,1,0:T(8,128)(2,1)S(1)} fusion(bf16[4,16,704]{2,1,0:T(8,128)(2,1)S(1)} %fusion.57, bf16[2,4,704,2048]{3,2,1,0:T(8,128)(2,1)} %param.14), kind=kOutput, calls=%fused_computation.34 | convolution fusion | flops 184680448 | bytes 11886592 | tf_op jit(solution)/shard_map/erf,efd->erd/dot_general | solution.py:56
  90.2 3.4 %all-to-all-start.4 = ((bf16[2,16,2,2048]{3,2,1,0:T(2,128)(2,1)}), bf16[2,16,2,2048]{3,2,1,0:T(2,128)(2,1)S(1)}, u32[]{:S(2)}, u32[]{:S(2)}) async-start(bf16[2,16,2,2048]{3,2,1,0:T(2,128)(2,1)} %bitcast.21), calls=%async_computation.4 | async-start | bytes 524288 | tf_op jit(solution)/shard_map/all_to_all | solution.py:64
  93.6 5.1 %all-to-all-done.4 = bf16[2,16,2,2048]{3,2,1,0:T(2,128)(2,1)S(1)} async-done(((bf16[2,16,2,2048]{3,2,1,0:T(2,128)(2,1)}), bf16[2,16,2,2048]{3,2,1,0:T(2,128)(2,1)S(1)}, u32[]{:S(2)}, u32[]{:S(2)}) %all-to-all-start.4) | async-done | bytes 262176 | tf_op jit(solution)/shard_map/all_to_all | solution.py:64
  99.9 3.5 %all-to-all-start.5 = ((bf16[16,2,2048]{2,1,0:T(2,128)(2,1)}), bf16[16,2,2048]{2,1,0:T(2,128)(2,1)S(1)}, u32[]{:S(2)}, u32[]{:S(2)}) async-start(bf16[16,2,2048]{2,1,0:T(2,128)(2,1)} %reduce_sum.181), calls=%async_computation.5 | async-start | bytes 262144 | tf_op jit(solution)/shard_map/all_to_all | solution.py:66
  103.6 5.6 %all-to-all-done.5 = bf16[16,2,2048]{2,1,0:T(2,128)(2,1)S(1)} async-done(((bf16[16,2,2048]{2,1,0:T(2,128)(2,1)}), bf16[16,2,2048]{2,1,0:T(2,128)(2,1)S(1)}, u32[]{:S(2)}, u32[]{:S(2)}) %all-to-all-start.5) | async-done | bytes 131104 | tf_op jit(solution)/shard_map/all_to_all | solution.py:66
  111.6 3.3 %all-to-all-start.6 = ((bf16[16,2,2048]{2,1,0:T(2,128)(2,1)}), bf16[16,2,2048]{2,1,0:T(2,128)(2,1)S(1)}, u32[]{:S(2)}, u32[]{:S(2)}) async-start(bf16[16,2,2048]{2,1,0:T(2,128)(2,1)} %reshape.319), calls=%async_computation.6 | async-start | bytes 262144 | tf_op jit(solution)/shard_map/all_to_all | solution.py:43
  116.2 4.6 %all-to-all-done.6 = bf16[16,2,2048]{2,1,0:T(2,128)(2,1)S(1)} async-done(((bf16[16,2,2048]{2,1,0:T(2,128)(2,1)}), bf16[16,2,2048]{2,1,0:T(2,128)(2,1)S(1)}, u32[]{:S(2)}, u32[]{:S(2)}) %all-to-all-start.6) | async-done | bytes 131104 | tf_op jit(solution)/shard_map/all_to_all | solution.py:43
  120.9 5.6 %all-gather.2 = bf16[32,2,2048]{2,1,0:T(2,128)(2,1)S(1)} all-gather(bf16[16,2,2048]{2,1,0:T(2,128)(2,1)S(1)} %all-to-all-done.6), channel_id=4, replica_groups=mesh['groups'=2,'expert'=4,'dp'=2,'mp'=2] {'dp'}, dimensions={0}, use_global_device_ids=true | all-gather | bytes 393216 | tf_op jit(solution)/shard_map/all_gather | solution.py:44
  126.8 6.0 %fusion.69 = bf16[4,16,704]{2,1,0:T(8,128)(2,1)S(1)} fusion(bf16[4,16,2048]{2,1,0:T(8,128)(2,1)S(1)} %reshape.321, bf16[2,4,2048,704]{2,3,1,0:T(8,128)(2,1)} %param.13), kind=kOutput, calls=%fused_computation.75 | convolution fusion | flops 184954880 | bytes 11886592 | tf_op jit(solution)/shard_map/erd,edf->erf/dot_general | solution.py:53
  132.8 5.9 %fusion.27 = bf16[4,16,2048]{2,1,0:T(8,128)(2,1)S(1)} fusion(bf16[4,16,704]{2,1,0:T(8,128)(2,1)S(1)} %fusion.69, bf16[2,4,704,2048]{3,2,1,0:T(8,128)(2,1)} %param.14), kind=kOutput, calls=%fused_computation.33 | convolution fusion | flops 184680448 | bytes 11886592 | tf_op jit(solution)/shard_map/erf,efd->erd/dot_general | solution.py:56
  139.8 3.4 %all-to-all-start.7 = ((bf16[2,16,2,2048]{3,2,1,0:T(2,128)(2,1)}), bf16[2,16,2,2048]{3,2,1,0:T(2,128)(2,1)S(1)}, u32[]{:S(2)}, u32[]{:S(2)}) async-start(bf16[2,16,2,2048]{3,2,1,0:T(2,128)(2,1)} %bitcast.29), calls=%async_computation.7 | async-start | bytes 524288 | tf_op jit(solution)/shard_map/all_to_all | solution.py:64
  143.3 5.1 %all-to-all-done.7 = bf16[2,16,2,2048]{3,2,1,0:T(2,128)(2,1)S(1)} async-done(((bf16[2,16,2,2048]{3,2,1,0:T(2,128)(2,1)}), bf16[2,16,2,2048]{3,2,1,0:T(2,128)(2,1)S(1)}, u32[]{:S(2)}, u32[]{:S(2)}) %all-to-all-start.7) | async-done | bytes 262176 | tf_op jit(solution)/shard_map/all_to_all | solution.py:64
  153.0 5.8 %all-to-all-done.8 = bf16[16,2,2048]{2,1,0:T(2,128)(2,1)S(1)} async-done(((bf16[16,2,2048]{2,1,0:T(2,128)(2,1)}), bf16[16,2,2048]{2,1,0:T(2,128)(2,1)S(1)}, u32[]{:S(2)}, u32[]{:S(2)}) %all-to-all-start.8) | async-done | bytes 131104 | tf_op jit(solution)/shard_map/all_to_all | solution.py:66
  165.8 4.6 %all-to-all-done.9 = bf16[16,2,2048]{2,1,0:T(2,128)(2,1)S(1)} async-done(((bf16[16,2,2048]{2,1,0:T(2,128)(2,1)}), bf16[16,2,2048]{2,1,0:T(2,128)(2,1)S(1)}, u32[]{:S(2)}, u32[]{:S(2)}) %all-to-all-start.9) | async-done | bytes 131104 | tf_op jit(solution)/shard_map/all_to_all | solution.py:43
  170.5 5.6 %all-gather.3 = bf16[32,2,2048]{2,1,0:T(2,128)(2,1)S(1)} all-gather(bf16[16,2,2048]{2,1,0:T(2,128)(2,1)S(1)} %all-to-all-done.9), channel_id=5, replica_groups=mesh['groups'=2,'expert'=4,'dp'=2,'mp'=2] {'dp'}, dimensions={0}, use_global_device_ids=true | all-gather | bytes 393216 | tf_op jit(solution)/shard_map/all_gather | solution.py:44
  176.4 6.0 %fusion.81 = bf16[4,16,704]{2,1,0:T(8,128)(2,1)S(1)} fusion(bf16[4,16,2048]{2,1,0:T(8,128)(2,1)S(1)} %reshape.327, bf16[2,4,2048,704]{2,3,1,0:T(8,128)(2,1)} %param.13), kind=kOutput, calls=%fused_computation.83 | convolution fusion | flops 184954880 | bytes 11886592 | tf_op jit(solution)/shard_map/erd,edf->erf/dot_general | solution.py:53
  182.4 5.9 %fusion.33 = bf16[4,16,2048]{2,1,0:T(8,128)(2,1)S(1)} fusion(bf16[4,16,704]{2,1,0:T(8,128)(2,1)S(1)} %fusion.81, bf16[2,4,704,2048]{3,2,1,0:T(8,128)(2,1)} %param.14), kind=kOutput, calls=%fused_computation.35 | convolution fusion | flops 184680448 | bytes 11886592 | tf_op jit(solution)/shard_map/erf,efd->erd/dot_general | solution.py:56
  189.4 3.4 %all-to-all-start.10 = ((bf16[2,16,2,2048]{3,2,1,0:T(2,128)(2,1)}), bf16[2,16,2,2048]{3,2,1,0:T(2,128)(2,1)S(1)}, u32[]{:S(2)}, u32[]{:S(2)}) async-start(bf16[2,16,2,2048]{3,2,1,0:T(2,128)(2,1)} %bitcast.37), calls=%async_computation.10 | async-start | bytes 524288 | tf_op jit(solution)/shard_map/all_to_all | solution.py:64
  192.9 5.1 %all-to-all-done.10 = bf16[2,16,2,2048]{3,2,1,0:T(2,128)(2,1)S(1)} async-done(((bf16[2,16,2,2048]{3,2,1,0:T(2,128)(2,1)}), bf16[2,16,2,2048]{3,2,1,0:T(2,128)(2,1)S(1)}, u32[]{:S(2)}, u32[]{:S(2)}) %all-to-all-start.10) | async-done | bytes 262176 | tf_op jit(solution)/shard_map/all_to_all | solution.py:64
  202.6 5.8 %all-to-all-done.11 = bf16[16,2,2048]{2,1,0:T(2,128)(2,1)S(1)} async-done(((bf16[16,2,2048]{2,1,0:T(2,128)(2,1)}), bf16[16,2,2048]{2,1,0:T(2,128)(2,1)S(1)}, u32[]{:S(2)}, u32[]{:S(2)}) %all-to-all-start.11) | async-done | bytes 131104 | tf_op jit(solution)/shard_map/all_to_all | solution.py:66
  (157 shorter events, 48.8 us)
Async XLA Ops:
  0.6 53.0 %copy-start.2 = (f32[2048]{0:T(1024)S(1)}, f32[2048]{0:T(1024)}, u32[]{:S(2)}) copy-start(f32[2048]{0:T(1024)} %param.10) | copy-start | bytes 24580
  0.6 60.2 %copy-start = (f32[16,2048]{1,0:T(8,128)S(1)}, f32[16,2048]{1,0:T(8,128)}, u32[]{:S(2)}) copy-start(f32[16,2048]{1,0:T(8,128)} %param.9) | copy-start | bytes 393220
  0.7 64.7 %copy-start.1 = (f32[2,2048,16]{1,2,0:T(8,128)S(1)}, f32[2,2048,16]{1,2,0:T(8,128)}, u32[]{:S(2)}) copy-start(f32[2,2048,16]{1,2,0:T(8,128)} %param.12) | copy-start | bytes 786436
  8.7 12.4 %all-to-all-start = ((bf16[16,2,2048]{2,1,0:T(2,128)(2,1)}), bf16[16,2,2048]{2,1,0:T(2,128)(2,1)S(1)}, u32[]{:S(2)}, u32[]{:S(2)}) async-start(bf16[16,2,2048]{2,1,0:T(2,128)(2,1)} %reshape.307), calls=%async_computation | async-start | bytes 262144 | tf_op jit(solution)/shard_map/all_to_all | solution.py:43
  39.0 54.6 %copy-start.3 = (s32[2,2,16,2]{2,3,1,0:T(2,128)S(1)}, s32[2,2,16,2]{2,3,1,0:T(2,128)}, u32[]{:S(2)}) copy-start(s32[2,2,16,2]{2,3,1,0:T(2,128)} %param.15) | copy-start | bytes 1540
  40.1 8.6 %all-to-all-start.1 = ((bf16[2,16,2,2048]{3,2,1,0:T(2,128)(2,1)}), bf16[2,16,2,2048]{3,2,1,0:T(2,128)(2,1)S(1)}, u32[]{:S(2)}, u32[]{:S(2)}) async-start(bf16[2,16,2,2048]{3,2,1,0:T(2,128)(2,1)} %bitcast.9), calls=%async_computation.1 | async-start | bytes 524288 | tf_op jit(solution)/shard_map/all_to_all | solution.py:64
  49.9 9.6 %all-to-all-start.2 = ((bf16[16,2,2048]{2,1,0:T(2,128)(2,1)}), bf16[16,2,2048]{2,1,0:T(2,128)(2,1)S(1)}, u32[]{:S(2)}, u32[]{:S(2)}) async-start(bf16[16,2,2048]{2,1,0:T(2,128)(2,1)} %reduce_sum.175), calls=%async_computation.2 | async-start | bytes 262144 | tf_op jit(solution)/shard_map/all_to_all | solution.py:66
  62.0 9.2 %all-to-all-start.3 = ((bf16[16,2,2048]{2,1,0:T(2,128)(2,1)}), bf16[16,2,2048]{2,1,0:T(2,128)(2,1)S(1)}, u32[]{:S(2)}, u32[]{:S(2)}) async-start(bf16[16,2,2048]{2,1,0:T(2,128)(2,1)} %reshape.313), calls=%async_computation.3 | async-start | bytes 262144 | tf_op jit(solution)/shard_map/all_to_all | solution.py:43
  90.2 8.6 %all-to-all-start.4 = ((bf16[2,16,2,2048]{3,2,1,0:T(2,128)(2,1)}), bf16[2,16,2,2048]{3,2,1,0:T(2,128)(2,1)S(1)}, u32[]{:S(2)}, u32[]{:S(2)}) async-start(bf16[2,16,2,2048]{3,2,1,0:T(2,128)(2,1)} %bitcast.21), calls=%async_computation.4 | async-start | bytes 524288 | tf_op jit(solution)/shard_map/all_to_all | solution.py:64
  99.9 9.2 %all-to-all-start.5 = ((bf16[16,2,2048]{2,1,0:T(2,128)(2,1)}), bf16[16,2,2048]{2,1,0:T(2,128)(2,1)S(1)}, u32[]{:S(2)}, u32[]{:S(2)}) async-start(bf16[16,2,2048]{2,1,0:T(2,128)(2,1)} %reduce_sum.181), calls=%async_computation.5 | async-start | bytes 262144 | tf_op jit(solution)/shard_map/all_to_all | solution.py:66
  111.6 9.2 %all-to-all-start.6 = ((bf16[16,2,2048]{2,1,0:T(2,128)(2,1)}), bf16[16,2,2048]{2,1,0:T(2,128)(2,1)S(1)}, u32[]{:S(2)}, u32[]{:S(2)}) async-start(bf16[16,2,2048]{2,1,0:T(2,128)(2,1)} %reshape.319), calls=%async_computation.6 | async-start | bytes 262144 | tf_op jit(solution)/shard_map/all_to_all | solution.py:43
  139.8 8.6 %all-to-all-start.7 = ((bf16[2,16,2,2048]{3,2,1,0:T(2,128)(2,1)}), bf16[2,16,2,2048]{3,2,1,0:T(2,128)(2,1)S(1)}, u32[]{:S(2)}, u32[]{:S(2)}) async-start(bf16[2,16,2,2048]{3,2,1,0:T(2,128)(2,1)} %bitcast.29), calls=%async_computation.7 | async-start | bytes 524288 | tf_op jit(solution)/shard_map/all_to_all | solution.py:64
  149.6 9.2 %all-to-all-start.8 = ((bf16[16,2,2048]{2,1,0:T(2,128)(2,1)}), bf16[16,2,2048]{2,1,0:T(2,128)(2,1)S(1)}, u32[]{:S(2)}, u32[]{:S(2)}) async-start(bf16[16,2,2048]{2,1,0:T(2,128)(2,1)} %reduce_sum.187), calls=%async_computation.8 | async-start | bytes 262144 | tf_op jit(solution)/shard_map/all_to_all | solution.py:66
  161.3 9.2 %all-to-all-start.9 = ((bf16[16,2,2048]{2,1,0:T(2,128)(2,1)}), bf16[16,2,2048]{2,1,0:T(2,128)(2,1)S(1)}, u32[]{:S(2)}, u32[]{:S(2)}) async-start(bf16[16,2,2048]{2,1,0:T(2,128)(2,1)} %reshape.325), calls=%async_computation.9 | async-start | bytes 262144 | tf_op jit(solution)/shard_map/all_to_all | solution.py:43
  189.4 8.6 %all-to-all-start.10 = ((bf16[2,16,2,2048]{3,2,1,0:T(2,128)(2,1)}), bf16[2,16,2,2048]{3,2,1,0:T(2,128)(2,1)S(1)}, u32[]{:S(2)}, u32[]{:S(2)}) async-start(bf16[2,16,2,2048]{3,2,1,0:T(2,128)(2,1)} %bitcast.37), calls=%async_computation.10 | async-start | bytes 524288 | tf_op jit(solution)/shard_map/all_to_all | solution.py:64
  199.2 9.2 %all-to-all-start.11 = ((bf16[16,2,2048]{2,1,0:T(2,128)(2,1)}), bf16[16,2,2048]{2,1,0:T(2,128)(2,1)S(1)}, u32[]{:S(2)}, u32[]{:S(2)}) async-start(bf16[16,2,2048]{2,1,0:T(2,128)(2,1)} %reduce_sum.193), calls=%async_computation.11 | async-start | bytes 262144 | tf_op jit(solution)/shard_map/all_to_all | solution.py:66
where the time goes:
time: 213 us; the launch traced here: 211 us
  waiting for transfers between devices  58.3 us (27%)
  matrix products  51.7 us (24%)
  starting transfers between devices  43.9 us (21%)
  blocking collectives  22.5 us (11%)
  local copies, waits for them, and re-layouts  19.8 us (9%)
  other arithmetic  13.6 us (6%)
    dot_general x4, matrix products, local_block(): jnp.einsum('erd,edf->erf', grouped, up_layer, preferred_element_type=jnp....  24.1 us
    dot_general x4, matrix products, local_block(): jnp.einsum('erf,efd->erd', hidden, down_layer, preferred_element_type=jnp...  23.6 us
    all_to_all x4, waiting for transfers between devices, local_block(): lax.all_to_all(summed, 'expert', split_axis=0, concat_axis=0, tiled=True)  23.1 us
    all_gather x4, blocking collectives, local_block(): arrived = lax.all_gather(landed[None], 'dp', axis=0, tiled=True)  22.5 us
    all_to_all x4, waiting for transfers between devices, local_block(): lax.all_to_all(partial_value, 'dp', split_axis=0, concat_axis=0, tiled=True)  19.9 us
    all_to_all x4, starting transfers between devices, local_block(): lax.all_to_all(buffer, 'expert', split_axis=0, concat_axis=0, tiled=True)  16.3 us
    all_to_all x4, waiting for transfers between devices, local_block(): lax.all_to_all(buffer, 'expert', split_axis=0, concat_axis=0, tiled=True)  15.3 us
    all_to_all x4, starting transfers between devices, local_block(): lax.all_to_all(summed, 'expert', split_axis=0, concat_axis=0, tiled=True)  13.9 us
  transfers between devices with their start and end apart: 12, of which 12 were waited for; matrix products, arithmetic and copies ran while one was open for 4% of the time, Pallas kernels for 0%

commit v1 on v0

v1 whole, which is shorter than its diff:
```python
import math

import jax
import jax.numpy as jnp
from jax import lax
from jax.experimental import pallas as pl
from jax.experimental.pallas import tpu as pltpu
from jax.sharding import PartitionSpec as P

CAP = 2

epsilon = 1e-06
start_time = 1.0
step_size = -0.5

bf16 = jnp.bfloat16
f32 = jnp.float32
i32 = jnp.int32


def div(x, n):
    if n & (n - 1) == 0:
        return x >> (n.bit_length() - 1)
    return x // n


def rem(x, n):
    if n & (n - 1) == 0:
        return x & (n - 1)
    return x - (x // n) * n


class Plan:
    def __init__(self, mesh, tokens, width, experts, local_experts):
        n_mp = mesh.shape["mp"]
        self.share = n_mp if local_experts % n_mp == 0 else 1
        self.axes = ("expert", "dp", "mp") if self.share > 1 else ("expert", "dp")
        self.n_dp = mesh.shape["dp"]
        self.peers = mesh.shape["expert"] * self.n_dp * self.share
        self.tokens = tokens
        self.width = width
        self.experts = experts
        self.local_experts = local_experts
        self.mine = local_experts // self.share
        self.rows = self.mine * CAP
        self.parts = 8 // math.gcd(8, self.rows)
        self.piece = width // self.parts
        self.block = self.rows * self.parts
        self.total = self.peers * self.block

    def where(self, index):
        peer = div(index, self.block)
        inner = rem(index, self.block)
        part = div(inner, self.rows)
        row = rem(inner, self.rows)
        expert = div(peer, self.n_dp * self.share) * self.local_experts
        if self.share > 1:
            expert = expert + rem(peer, self.share) * self.mine
        return part, expert + div(row, CAP), rem(row, CAP)


def column(row, tokens):
    eye = lax.broadcasted_iota(i32, (tokens, tokens), 0) == lax.broadcasted_iota(
        i32, (tokens, tokens), 1
    )
    return jnp.sum(jnp.where(eye, row, 0), axis=1, keepdims=True)


def dispatch_select(plan, first, second):
    shape = (plan.total, plan.tokens)
    part, expert, slot = plan.where(lax.broadcasted_iota(i32, shape, 0))
    named = jnp.where((first == expert) | (second == expert), 1.0, 0.0)
    earlier = jnp.where(
        lax.broadcasted_iota(i32, (plan.tokens, plan.tokens), 0)
        < lax.broadcasted_iota(i32, (plan.tokens, plan.tokens), 1),
        1.0,
        0.0,
    ).astype(bf16)
    before = jnp.dot(named.astype(bf16), earlier, preferred_element_type=f32)
    chosen = jnp.where(before == slot.astype(f32), named, 0.0)
    return [jnp.where(part == p, chosen, 0.0).astype(bf16) for p in range(plan.parts)]


def combine_select(plan, first, second, mix):
    shape = (plan.tokens, plan.total)
    part, expert, slot = plan.where(lax.broadcasted_iota(i32, shape, 1))
    is_first = first == expert
    is_second = second == expert
    named = jnp.where(is_first | is_second, 1.0, 0.0)
    earlier = jnp.where(
        lax.broadcasted_iota(i32, (plan.tokens, plan.tokens), 1)
        < lax.broadcasted_iota(i32, (plan.tokens, plan.tokens), 0),
        1.0,
        0.0,
    ).astype(bf16)
    before = jnp.dot(earlier, named.astype(bf16), preferred_element_type=f32)
    weight = jnp.where(is_first, mix, 0.0) + jnp.where(is_second, 1.0 - mix, 0.0)
    return jnp.where(before == slot.astype(f32), weight, 0.0)


def combine(plan, state, weight, returned):
    part, _, _ = plan.where(lax.broadcasted_iota(i32, weight.shape, 1))
    high = weight.astype(bf16).astype(f32)
    middle = (weight - high).astype(bf16).astype(f32)
    low = weight - high - middle
    stacked = jnp.concatenate(
        [
            jnp.where(part == p, term, 0.0)
            for p in range(plan.parts)
            for term in (high, middle, low)
        ],
        axis=0,
    ).astype(bf16)
    product = jnp.dot(stacked, returned, preferred_element_type=f32)
    t = plan.tokens
    pieces = []
    for p in range(plan.parts):
        base = 3 * t * p
        pieces.append(
            product[base : base + t]
            + product[base + t : base + 2 * t]
            + product[base + 2 * t : base + 3 * t]
        )
    return state + jnp.concatenate(pieces, axis=1)


def emit_dispatch(plan, state, gain, router, routes, slots_ref, weight_ref):
    inverse = lax.rsqrt(jnp.mean(state * state, axis=1, keepdims=True) + epsilon)
    scaled = state * inverse * gain
    normed = scaled.astype(bf16)
    first = routes[0:1]
    second = routes[1:2]
    select = dispatch_select(plan, first, second)
    sent = jnp.zeros((plan.total, plan.piece), f32)
    for p in range(plan.parts):
        sent = sent + jnp.dot(
            select[p],
            normed[:, p * plan.piece : (p + 1) * plan.piece],
            preferred_element_type=f32,
        )
    slots_ref[...] = sent.astype(bf16)
    logits = lax.dot_general(
        scaled,
        router,
        (((1,), (1,)), ((), ())),
        precision=lax.Precision.HIGHEST,
        preferred_element_type=f32,
    )
    first_column = column(first, plan.tokens)
    second_column = column(second, plan.tokens)
    lane = lax.broadcasted_iota(i32, (plan.tokens, plan.experts), 1)
    gap = jnp.sum(
        jnp.where(lane == first_column, logits, 0.0)
        - jnp.where(lane == second_column, logits, 0.0),
        axis=1,
        keepdims=True,
    )
    mix = jax.nn.sigmoid(gap)
    weight_ref[...] = combine_select(plan, first_column, second_column, mix)


def per_device_fn(mesh):
    vmem = pl.BlockSpec(memory_space=pltpu.VMEM)

    def run(latent, time_embedding, norm_gain, router, up_proj, down_proj, routes):
        tokens, width = latent.shape
        layers, _, experts = router.shape
        local_experts = up_proj.shape[1]
        hidden = up_proj.shape[3]
        plan = Plan(mesh, tokens, width, experts, local_experts)
        mine = plan.mine

        embedding = time_embedding.reshape(1, width)
        router_t = jnp.swapaxes(router, 1, 2)
        routes_t = jnp.swapaxes(routes, 2, 3)

        def call(body, outs, args, **kw):
            return pl.pallas_call(
                body,
                out_shape=outs,
                in_specs=[vmem] * len(args),
                out_specs=[vmem] * len(outs),
                compiler_params=pltpu.CompilerParams(vmem_limit_bytes=16 << 20),
                **kw,
            )(*args)

        state_shape = jax.ShapeDtypeStruct((tokens, width), f32)
        slots_shape = pltpu.VMEM((plan.total, plan.piece), bf16)
        weight_shape = pltpu.VMEM((tokens, plan.total), f32)

        def begin(step, layer):
            def body(latent_ref, emb_ref, gain_ref, router_ref, routes_ref, state_ref, slots_ref, weight_ref):
                state = latent_ref[...] + start_time * emb_ref[...]
                state_ref[...] = state
                emit_dispatch(
                    plan, state, gain_ref[layer : layer + 1], router_ref[layer],
                    routes_ref[step, layer], slots_ref, weight_ref,
                )

            return call(
                body, [state_shape, slots_shape, weight_shape],
                [latent, embedding, norm_gain, router_t, routes_t],
            )

        def middle(step, layer, state, weight, returned):
            def body(state_in, weight_in, returned_ref, gain_ref, router_ref, routes_ref, state_ref, slots_ref, weight_ref):
                state = combine(plan, state_in[...], weight_in[...], returned_ref[...])
                state_ref[...] = state
                emit_dispatch(
                    plan, state, gain_ref[layer : layer + 1], router_ref[layer],
                    routes_ref[step, layer], slots_ref, weight_ref,
                )

            return call(
                body, [state_shape, slots_shape, weight_shape],
                [state, weight, returned, norm_gain, router_t, routes_t],
            )

        def turn(step, layer, state, weight, returned):
            def body(latent_ref, emb_ref, state_in, weight_in, returned_ref, gain_ref, router_ref, routes_ref,
                     first_ref, state_ref, slots_ref, weight_ref):
                state = combine(plan, state_in[...], weight_in[...], returned_ref[...])
                first = state - latent_ref[...]
                first_ref[...] = first
                moved = latent_ref[...] + step_size * first
                state = moved + (start_time + step_size) * emb_ref[...]
                state_ref[...] = state
                emit_dispatch(
                    plan, state, gain_ref[layer : layer + 1], router_ref[layer],
                    routes_ref[step, layer], slots_ref, weight_ref,
                )

            return call(
                body, [state_shape, state_shape, slots_shape, weight_shape],
                [latent, embedding, state, weight, returned, norm_gain, router_t, routes_t],
            )

        def finish(state, weight, returned, first):
            def body(latent_ref, state_in, weight_in, returned_ref, first_ref, next_ref, mean_ref):
                state = combine(plan, state_in[...], weight_in[...], returned_ref[...])
                first = first_ref[...]
                moved = latent_ref[...] + step_size * first
                mean = 0.5 * (first + (state - moved))
                mean_ref[...] = mean
                next_ref[...] = latent_ref[...] + step_size * mean

            return call(body, [state_shape, state_shape], [latent, state, weight, returned, first])

        def load(layer):
            def body(up_ref, down_ref, up_out, down_out, sems):
                base = lax.axis_index("mp") * mine if plan.share > 1 else 0
                a = pltpu.make_async_copy(up_ref.at[layer, pl.ds(base, mine)], up_out, sems.at[0])
                b = pltpu.make_async_copy(down_ref.at[layer, pl.ds(base, mine)], down_out, sems.at[1])
                a.start()
                b.start()
                a.wait()
                b.wait()

            return pl.pallas_call(
                body,
                out_shape=[
                    pltpu.VMEM((mine, width, hidden), bf16),
                    pltpu.VMEM((mine, hidden, width), bf16),
                ],
                in_specs=[pl.BlockSpec(memory_space=pl.ANY)] * 2,
                out_specs=[vmem] * 2,
                scratch_shapes=[pltpu.SemaphoreType.DMA((2,))],
                compiler_params=pltpu.CompilerParams(vmem_limit_bytes=2 << 20),
            )(up_proj, down_proj)

        each = plan.peers * CAP

        def experts_body(arrived_ref, up_ref, down_ref, out_ref):
            total = plan.rows * plan.peers

            def picks(shape, row_axis):
                row = lax.broadcasted_iota(i32, shape, row_axis)
                piece = lax.broadcasted_iota(i32, shape, 1 - row_axis)
                local = div(row, each)
                source = div(rem(row, each), CAP)
                target = source * plan.block + local * CAP + rem(row, CAP)
                return [
                    jnp.where(piece == target + p * plan.rows, 1.0, 0.0).astype(bf16)
                    for p in range(plan.parts)
                ]

            arrived = arrived_ref[...]
            rows = jnp.concatenate(
                [
                    jnp.dot(pick, arrived, preferred_element_type=f32).astype(bf16)
                    for pick in picks((total, plan.total), 0)
                ],
                axis=1,
            )
            results = []
            for local in range(mine):
                own = rows[local * each : (local + 1) * each]
                hid = jax.nn.gelu(
                    jnp.dot(own, up_ref[local], preferred_element_type=f32), approximate=True
                ).astype(bf16)
                results.append(jnp.dot(hid, down_ref[local], preferred_element_type=f32).astype(bf16))
            result = jnp.concatenate(results, axis=0)
            out = jnp.zeros((plan.total, plan.piece), f32)
            for p, pick in enumerate(picks((plan.total, total), 1)):
                out = out + jnp.dot(
                    pick, result[:, p * plan.piece : (p + 1) * plan.piece], preferred_element_type=f32
                )
            out_ref[...] = out.astype(bf16)

        def compute(arrived, layer_weights):
            return call(experts_body, [slots_shape], [arrived, *layer_weights])[0]

        def exchange(x):
            return lax.all_to_all(x, plan.axes, split_axis=0, concat_axis=0, tiled=True)

        state, slots, weight = begin(0, 0)
        loaded = [load(layer) for layer in range(layers)]
        first = None
        for step in range(2):
            for layer in range(layers):
                returned = exchange(compute(exchange(slots), loaded[layer]))
                if layer + 1 < layers:
                    state, slots, weight = middle(step, layer + 1, state, weight, returned)
                elif step == 0:
                    first, state, slots, weight = turn(1, 0, state, weight, returned)
                else:
                    return tuple(finish(state, weight, returned, first))

    return run


def solution(mesh):
    placed = (
        P(("groups", "expert", "dp", "mp"), None),
        P(),
        P(),
        P(),
        P(None, "expert", None, "dp"),
        P(None, "expert", "dp", None),
        P(None, None, ("groups", "expert", "dp", "mp"), None),
    )
    return jax.shard_map(
        per_device_fn(mesh),
        mesh=mesh,
        in_specs=placed,
        out_specs=(
            P(("groups", "expert", "dp", "mp"), None),
            P(("groups", "expert", "dp", "mp"), None),
        ),
        check_vma=False,
    )
```

time: 213 us -> 191 us (0.90)
  blocking collectives: 22.5 us -> 82.8 us
  waiting for transfers between devices: 58.3 us -> 0.01 us
  local copies, waits for them, and re-layouts: 19.8 us -> 72.3 us
  matrix products: 51.7 us -> 0 us
  starting transfers between devices: 43.9 us -> 10.9 us
  Pallas kernels: 0 us -> 22.6 us
  other arithmetic: 13.6 us -> 0.01 us
    all_to_all x0 -> x6, blocking collectives: none -> 82.8 us  [exchange(): return lax.all_to_all(x, plan.axes, split_axis=0, concat_axis=0, tiled=True)]
    unnamed x8 -> x49, local copies, waits for them, and re-layouts: 0.02 us -> 72.3 us
    all_to_all x12 -> x2, waiting for transfers between devices: 58.3 us -> 0.01 us  [exchange(): return lax.all_to_all(x, plan.axes, split_axis=0, concat_axis=0, tiled=True)]
    dot_general x16 -> x0, matrix products: 51.7 us -> none  [the longest x4 24.1 us: local_block(): jnp.einsum('erd,edf->erf', grouped, up_layer, preferred_element_type=jnp....]
    all_to_all x12 -> x2, starting transfers between devices: 43.9 us -> 10.9 us  [exchange(): return lax.all_to_all(x, plan.axes, split_axis=0, concat_axis=0, tiled=True)]
    pallas_call x0 -> x11, Pallas kernels: none -> 22.6 us  [the longest x9 17 us: call(): pl.pallas_call(body, out_shape=outs, in_specs=[vmem] * len(args), out_spe...]
    all_gather x4 -> x0, blocking collectives: 22.5 us -> none  [local_block(): arrived = lax.all_gather(landed[None], 'dp', axis=0, tiled=True)]
    reshape x24 -> x0, local copies, waits for them, and re-layouts: 8.75 us -> none  [the longest x8 4.33 us: local_block(): partial_value.reshape(local_experts, group_count, source_count, CAP, mode...]
  transfers between devices with their start and end apart: 12 -> 2, of which waited for: 12 -> 0; matrix products, arithmetic and copies ran while one was open for 4% -> 17% of each run, Pallas kernels for 0% -> 3%
where the time goes in v1:
time: 191 us; the launch traced here: 189 us
  blocking collectives  82.8 us (43%)
  local copies, waits for them, and re-layouts  72.3 us (38%)
  Pallas kernels  22.6 us (12%)
  starting transfers between devices  10.9 us (6%)
    all_to_all x6, blocking collectives, exchange(): return lax.all_to_all(x, plan.axes, split_axis=0, concat_axis=0, tiled=True)  82.8 us
    unnamed x49, local copies, waits for them, and re-layouts  72.3 us
    pallas_call x9, Pallas kernels, call(): pl.pallas_call(body, out_shape=outs, in_specs=[vmem] * len(args), out_spe...  17 us
    all_to_all x2, starting transfers between devices, exchange(): return lax.all_to_all(x, plan.axes, split_axis=0, concat_axis=0, tiled=True)  10.9 us
    pallas_call x2, Pallas kernels, load(): pl.pallas_call(body, out_shape=[pltpu.VMEM((mine, width, hidden), bf16),...  5.61 us
  transfers between devices with their start and end apart: 2, of which 0 were waited for; matrix products, arithmetic and copies ran while one was open for 17% of the time, Pallas kernels for 3%

profile of v1, /device:TPU:0, one launch (start us, length us, event | category | flops | bytes accessed | tf_op | source)
XLA Modules:
  0.0 189.4 jit_solution(13416328747035008037)
XLA Ops:
  0.6 0.9 copy-done.12
  1.6 0.9 copy-done.14
  4.6 1.3 shard_map.86
  5.9 7.4 %all-to-all-start = ((bf16[16,8,1024]{2,1,0:T(8,128)(2,1)}), bf16[16,8,1024]{2,1,0:T(8,128)(2,1)S(1)}, u32[]{:S(2)}, u32[]{:S(2)}) async-start(bf16[16,8,1024]{2,1,0:T(8,128)(2,1)} %bitcast.3), calls=%async_computation | async-start | bytes 524288 | tf_op jit(solution)/shard_map/all_to_all | solution.py:314
  13.3 32.1 %copy.9.up_ref = bf16[2,4,2048,704]{3,2,1,0:T(8,128)(2,1)} copy(bf16[2,4,2048,704]{2,3,1,0:T(8,128)(2,1)} %param.11) | data formatting | bytes 46137344 | tf_op args[4]
  45.4 7.6 %copy-done = bf16[2,4,704,2048]{3,2,1,0:T(8,128)(2,1)S(1)} copy-done((bf16[2,4,704,2048]{3,2,1,0:T(8,128)(2,1)S(1)}, bf16[2,4,704,2048]{3,2,1,0:T(8,128)(2,1)}, u32[]{:S(2)}) %copy-start) | copy-done | bytes 23068696
  52.9 2.8 %shard_map.87 = (bf16[2,2048,704]{2,1,0:T(8,128)(2,1)S(1)}, bf16[2,704,2048]{2,1,0:T(8,128)(2,1)S(1)}) custom-call(bf16[2,4,2048,704]{3,2,1,0:T(8,128)(2,1)} %copy.9.up_ref, bf16[2,4,704,2048]{3,2,1,0:T(8,128)(2,1)S(1)} %copy-done), custom_call_target="tpu_custom_call" | custom-call | tf_op jit(solution)/shard_map/pallas_call | solution.py:259
  55.7 2.7 %copy-done.2 = bf16[2,2048,704]{2,1,0:T(8,128)(2,1)} copy-done((bf16[2,2048,704]{2,1,0:T(8,128)(2,1)}, bf16[2,2048,704]{2,1,0:T(8,128)(2,1)S(1)}, u32[]{:S(2)}) %copy-start.2) | copy-done | bytes 5767192
  58.4 2.5 %copy-done.7 = bf16[2,704,2048]{2,1,0:T(8,128)(2,1)} copy-done((bf16[2,704,2048]{2,1,0:T(8,128)(2,1)}, bf16[2,704,2048]{2,1,0:T(8,128)(2,1)S(1)}, u32[]{:S(2)}) %copy-start.7) | copy-done | bytes 5767192
  61.0 2.8 %copy-done.3 = bf16[2,2048,704]{2,1,0:T(8,128)(2,1)S(1)} copy-done((bf16[2,2048,704]{2,1,0:T(8,128)(2,1)S(1)}, bf16[2,2048,704]{2,1,0:T(8,128)(2,1)}, u32[]{:S(2)}) %copy-start.3) | copy-done | bytes 5767192
  63.8 2.6 %copy-done.8 = bf16[2,704,2048]{2,1,0:T(8,128)(2,1)S(1)} copy-done((bf16[2,704,2048]{2,1,0:T(8,128)(2,1)S(1)}, bf16[2,704,2048]{2,1,0:T(8,128)(2,1)}, u32[]{:S(2)}) %copy-start.8) | copy-done | bytes 5767192
  66.4 2.9 %shard_map.88 = bf16[128,1024]{1,0:T(8,128)(2,1)S(1)} custom-call(bf16[128,1024]{1,0:T(8,128)(2,1)S(1)} %bitcast.25, bf16[2,2048,704]{2,1,0:T(8,128)(2,1)S(1)} %copy-done.3, bf16[2,704,2048]{2,1,0:T(8,128)(2,1)S(1)} %copy-done.8), custom_call_target="tpu_custom_call" | custom-call | tf_op jit(solution)/shard_map/pallas_call | solution.py:178
  69.3 15.8 %all_to_all.88 = bf16[16,8,1024]{2,1,0:T(8,128)(2,1)S(1)} all-to-all(bf16[16,8,1024]{2,1,0:T(8,128)(2,1)S(1)} %bitcast.32), channel_id=1, replica_groups=mesh['groups'=2,'expert'=4,'dp'=2,'mp'=2] {'expert','dp','mp'}, dimensions={0} | all-to-all | bytes 524288 | tf_op jit(solution)/shard_map/all_to_all | solution.py:314
  85.1 1.5 shard_map.89
  86.6 3.5 %all-to-all-start.2 = ((bf16[16,8,1024]{2,1,0:T(8,128)(2,1)}), bf16[16,8,1024]{2,1,0:T(8,128)(2,1)S(1)}, u32[]{:S(2)}, u32[]{:S(2)}) async-start(bf16[16,8,1024]{2,1,0:T(8,128)(2,1)} %bitcast.7), calls=%async_computation.2 | async-start | bytes 524288 | tf_op jit(solution)/shard_map/all_to_all | solution.py:314
  90.1 7.6 %copy-done.1 = bf16[2,4,704,2048]{3,2,1,0:T(8,128)(2,1)S(1)} copy-done((bf16[2,4,704,2048]{3,2,1,0:T(8,128)(2,1)S(1)}, bf16[2,4,704,2048]{3,2,1,0:T(8,128)(2,1)}, u32[]{:S(2)}) %copy-start.1) | copy-done | bytes 23068696
  97.7 2.8 %shard_map.90 = (bf16[2,2048,704]{2,1,0:T(8,128)(2,1)S(1)}, bf16[2,704,2048]{2,1,0:T(8,128)(2,1)S(1)}) custom-call(bf16[2,4,2048,704]{3,2,1,0:T(8,128)(2,1)} %copy.9.up_ref, bf16[2,4,704,2048]{3,2,1,0:T(8,128)(2,1)S(1)} %copy-done.1), custom_call_target="tpu_custom_call" | custom-call | tf_op jit(solution)/shard_map/pallas_call | solution.py:259
  100.5 2.6 %copy-done.5 = bf16[2,2048,704]{2,1,0:T(8,128)(2,1)} copy-done((bf16[2,2048,704]{2,1,0:T(8,128)(2,1)}, bf16[2,2048,704]{2,1,0:T(8,128)(2,1)S(1)}, u32[]{:S(2)}) %copy-start.5) | copy-done | bytes 5767192
  103.1 2.4 %copy-done.10 = bf16[2,704,2048]{2,1,0:T(8,128)(2,1)} copy-done((bf16[2,704,2048]{2,1,0:T(8,128)(2,1)}, bf16[2,704,2048]{2,1,0:T(8,128)(2,1)S(1)}, u32[]{:S(2)}) %copy-start.10) | copy-done | bytes 5767192
  105.6 2.8 %copy-done.6 = bf16[2,2048,704]{2,1,0:T(8,128)(2,1)S(1)} copy-done((bf16[2,2048,704]{2,1,0:T(8,128)(2,1)S(1)}, bf16[2,2048,704]{2,1,0:T(8,128)(2,1)}, u32[]{:S(2)}) %copy-start.6) | copy-done | bytes 5767192
  108.3 2.6 %copy-done.11 = bf16[2,704,2048]{2,1,0:T(8,128)(2,1)S(1)} copy-done((bf16[2,704,2048]{2,1,0:T(8,128)(2,1)S(1)}, bf16[2,704,2048]{2,1,0:T(8,128)(2,1)}, u32[]{:S(2)}) %copy-start.11) | copy-done | bytes 5767192
  111.0 2.9 %shard_map.91 = bf16[128,1024]{1,0:T(8,128)(2,1)S(1)} custom-call(bf16[128,1024]{1,0:T(8,128)(2,1)S(1)} %bitcast.26, bf16[2,2048,704]{2,1,0:T(8,128)(2,1)S(1)} %copy-done.6, bf16[2,704,2048]{2,1,0:T(8,128)(2,1)S(1)} %copy-done.11), custom_call_target="tpu_custom_call" | custom-call | tf_op jit(solution)/shard_map/pallas_call | solution.py:178
  113.9 15.9 %all_to_all.89 = bf16[16,8,1024]{2,1,0:T(8,128)(2,1)S(1)} all-to-all(bf16[16,8,1024]{2,1,0:T(8,128)(2,1)S(1)} %bitcast.33), channel_id=1, replica_groups=mesh['groups'=2,'expert'=4,'dp'=2,'mp'=2] {'expert','dp','mp'}, dimensions={0} | all-to-all | bytes 524288 | tf_op jit(solution)/shard_map/all_to_all | solution.py:314
  129.8 1.0 shard_map.92
  130.7 12.9 %all_to_all.90 = bf16[16,8,1024]{2,1,0:T(8,128)(2,1)S(1)} all-to-all(bf16[16,8,1024]{2,1,0:T(8,128)(2,1)S(1)} %bitcast.37), channel_id=1, replica_groups=mesh['groups'=2,'expert'=4,'dp'=2,'mp'=2] {'expert','dp','mp'}, dimensions={0} | all-to-all | bytes 524288 | tf_op jit(solution)/shard_map/all_to_all | solution.py:314
  143.7 2.9 %shard_map.93 = bf16[128,1024]{1,0:T(8,128)(2,1)S(1)} custom-call(bf16[128,1024]{1,0:T(8,128)(2,1)S(1)} %bitcast.28, bf16[2,2048,704]{2,1,0:T(8,128)(2,1)S(1)} %copy-done.4, bf16[2,704,2048]{2,1,0:T(8,128)(2,1)S(1)} %copy-done.9), custom_call_target="tpu_custom_call" | custom-call | tf_op jit(solution)/shard_map/pallas_call | solution.py:178
  146.6 12.7 %all_to_all.91 = bf16[16,8,1024]{2,1,0:T(8,128)(2,1)S(1)} all-to-all(bf16[16,8,1024]{2,1,0:T(8,128)(2,1)S(1)} %bitcast.29), channel_id=1, replica_groups=mesh['groups'=2,'expert'=4,'dp'=2,'mp'=2] {'expert','dp','mp'}, dimensions={0} | all-to-all | bytes 524288 | tf_op jit(solution)/shard_map/all_to_all | solution.py:314
  159.3 0.9 shard_map.94
  160.2 12.7 %all_to_all.92 = bf16[16,8,1024]{2,1,0:T(8,128)(2,1)S(1)} all-to-all(bf16[16,8,1024]{2,1,0:T(8,128)(2,1)S(1)} %bitcast.38), channel_id=1, replica_groups=mesh['groups'=2,'expert'=4,'dp'=2,'mp'=2] {'expert','dp','mp'}, dimensions={0} | all-to-all | bytes 524288 | tf_op jit(solution)/shard_map/all_to_all | solution.py:314
  172.9 2.9 %shard_map.95 = bf16[128,1024]{1,0:T(8,128)(2,1)S(1)} custom-call(bf16[128,1024]{1,0:T(8,128)(2,1)S(1)} %bitcast.30, bf16[2,2048,704]{2,1,0:T(8,128)(2,1)S(1)} %bitcast.20, bf16[2,704,2048]{2,1,0:T(8,128)(2,1)S(1)} %copy-done.11), custom_call_target="tpu_custom_call" | custom-call | tf_op jit(solution)/shard_map/pallas_call | solution.py:178
  175.8 12.7 %all_to_all.93 = bf16[16,8,1024]{2,1,0:T(8,128)(2,1)S(1)} all-to-all(bf16[16,8,1024]{2,1,0:T(8,128)(2,1)S(1)} %bitcast.31), channel_id=1, replica_groups=mesh['groups'=2,'expert'=4,'dp'=2,'mp'=2] {'expert','dp','mp'}, dimensions={0} | all-to-all | bytes 524288 | tf_op jit(solution)/shard_map/all_to_all | solution.py:314
  188.5 0.9 shard_map.96
  (39 shorter events, 2.2 us)
Async XLA Ops:
  0.6 1.0 copy-start.12
  1.6 0.9 copy-start.14
  2.5 0.7 copy-start.16
  3.2 0.7 copy-start.18
  3.9 0.7 copy-start.20
  5.9 55.1 %all-to-all-start = ((bf16[16,8,1024]{2,1,0:T(8,128)(2,1)}), bf16[16,8,1024]{2,1,0:T(8,128)(2,1)S(1)}, u32[]{:S(2)}, u32[]{:S(2)}) async-start(bf16[16,8,1024]{2,1,0:T(8,128)(2,1)} %bitcast.3), calls=%async_computation | async-start | bytes 524288 | tf_op jit(solution)/shard_map/all_to_all | solution.py:314
  45.4 7.6 %copy-start = (bf16[2,4,704,2048]{3,2,1,0:T(8,128)(2,1)S(1)}, bf16[2,4,704,2048]{3,2,1,0:T(8,128)(2,1)}, u32[]{:S(2)}) copy-start(bf16[2,4,704,2048]{3,2,1,0:T(8,128)(2,1)} %down_ref.3) | copy-start | bytes 69206016
  55.7 2.7 %copy-start.2 = (bf16[2,2048,704]{2,1,0:T(8,128)(2,1)}, bf16[2,2048,704]{2,1,0:T(8,128)(2,1)S(1)}, u32[]{:S(2)}) copy-start(bf16[2,2048,704]{2,1,0:T(8,128)(2,1)S(1)} %get-tuple-element.22.up_ref) | copy-start | bytes 17301508
  58.4 2.5 %copy-start.7 = (bf16[2,704,2048]{2,1,0:T(8,128)(2,1)}, bf16[2,704,2048]{2,1,0:T(8,128)(2,1)S(1)}, u32[]{:S(2)}) copy-start(bf16[2,704,2048]{2,1,0:T(8,128)(2,1)S(1)} %get-tuple-element.23.down_ref) | copy-start | bytes 17301508
  61.0 2.8 %copy-start.3 = (bf16[2,2048,704]{2,1,0:T(8,128)(2,1)S(1)}, bf16[2,2048,704]{2,1,0:T(8,128)(2,1)}, u32[]{:S(2)}) copy-start(bf16[2,2048,704]{2,1,0:T(8,128)(2,1)} %copy-done.2) | copy-start | bytes 17301508
  63.7 2.6 %copy-start.8 = (bf16[2,704,2048]{2,1,0:T(8,128)(2,1)S(1)}, bf16[2,704,2048]{2,1,0:T(8,128)(2,1)}, u32[]{:S(2)}) copy-start(bf16[2,704,2048]{2,1,0:T(8,128)(2,1)} %copy-done.7) | copy-start | bytes 17301508
  66.4 18.7 %copy-start.13 = (f32[2,2048,16]{1,2,0:T(8,128)S(1)}, f32[2,2048,16]{1,2,0:T(8,128)}, u32[]{:S(2)}) copy-start(f32[2,2048,16]{1,2,0:T(8,128)} %param.10) | copy-start | bytes 786436
  66.4 18.7 %copy-start.17 = (f32[2,2048]{1,0:T(2,128)S(1)}, f32[2,2048]{1,0:T(2,128)}, u32[]{:S(2)}) copy-start(f32[2,2048]{1,0:T(2,128)} %gain_ref.7) | copy-start | bytes 49156
  66.4 18.7 %copy-start.19 = (s32[2,2,16,2]{2,3,1,0:T(2,128)S(1)}, s32[2,2,16,2]{2,3,1,0:T(2,128)}, u32[]{:S(2)}) copy-start(s32[2,2,16,2]{2,3,1,0:T(2,128)} %param.13) | copy-start | bytes 1540
  86.6 19.0 %all-to-all-start.2 = ((bf16[16,8,1024]{2,1,0:T(8,128)(2,1)}), bf16[16,8,1024]{2,1,0:T(8,128)(2,1)S(1)}, u32[]{:S(2)}, u32[]{:S(2)}) async-start(bf16[16,8,1024]{2,1,0:T(8,128)(2,1)} %bitcast.7), calls=%async_computation.2 | async-start | bytes 524288 | tf_op jit(solution)/shard_map/all_to_all | solution.py:314
  90.1 7.6 %copy-start.1 = (bf16[2,4,704,2048]{3,2,1,0:T(8,128)(2,1)S(1)}, bf16[2,4,704,2048]{3,2,1,0:T(8,128)(2,1)}, u32[]{:S(2)}) copy-start(bf16[2,4,704,2048]{3,2,1,0:T(8,128)(2,1)} %down_ref.3) | copy-start | bytes 69206016
  100.5 2.6 %copy-start.5 = (bf16[2,2048,704]{2,1,0:T(8,128)(2,1)}, bf16[2,2048,704]{2,1,0:T(8,128)(2,1)S(1)}, u32[]{:S(2)}) copy-start(bf16[2,2048,704]{2,1,0:T(8,128)(2,1)S(1)} %get-tuple-element.27.up_ref) | copy-start | bytes 17301508
  103.1 2.4 %copy-start.10 = (bf16[2,704,2048]{2,1,0:T(8,128)(2,1)}, bf16[2,704,2048]{2,1,0:T(8,128)(2,1)S(1)}, u32[]{:S(2)}) copy-start(bf16[2,704,2048]{2,1,0:T(8,128)(2,1)S(1)} %get-tuple-element.28.down_ref) | copy-start | bytes 17301508
  105.5 2.8 %copy-start.6 = (bf16[2,2048,704]{2,1,0:T(8,128)(2,1)S(1)}, bf16[2,2048,704]{2,1,0:T(8,128)(2,1)}, u32[]{:S(2)}) copy-start(bf16[2,2048,704]{2,1,0:T(8,128)(2,1)} %copy-done.5) | copy-start | bytes 17301508
  108.3 2.6 %copy-start.11 = (bf16[2,704,2048]{2,1,0:T(8,128)(2,1)S(1)}, bf16[2,704,2048]{2,1,0:T(8,128)(2,1)}, u32[]{:S(2)}) copy-start(bf16[2,704,2048]{2,1,0:T(8,128)(2,1)} %copy-done.10) | copy-start | bytes 17301508
  111.0 18.8 %copy-start.15 = (f32[16,2048]{1,0:T(8,128)S(1)}, f32[16,2048]{1,0:T(8,128)}, u32[]{:S(2)}) copy-start(f32[16,2048]{1,0:T(8,128)} %latent_ref.5) | copy-start | bytes 393220
  111.0 18.8 %copy-start.21 = (f32[2048]{0:T(1024)S(1)}, f32[2048]{0:T(1024)}, u32[]{:S(2)}) copy-start(f32[2048]{0:T(1024)} %param.8) | copy-start | bytes 24580
  111.0 32.7 %copy-start.4 = (bf16[2,2048,704]{2,1,0:T(8,128)(2,1)S(1)}, bf16[2,2048,704]{2,1,0:T(8,128)(2,1)}, u32[]{:S(2)}) copy-start(bf16[2,2048,704]{2,1,0:T(8,128)(2,1)} %copy-done.2) | copy-start | bytes 17301508
  111.0 32.7 %copy-start.9 = (bf16[2,704,2048]{2,1,0:T(8,128)(2,1)S(1)}, bf16[2,704,2048]{2,1,0:T(8,128)(2,1)}, u32[]{:S(2)}) copy-start(bf16[2,704,2048]{2,1,0:T(8,128)(2,1)} %copy-done.7) | copy-start | bytes 17301508
  130.7 42.2 %slice-start = ((s8[6291456]{0:T(1024)(128)(4,1)}), s8[4194304]{0:T(1024)(128)(4,1)S(1)}, s32[]{:S(2)}) async-start(s8[6291456]{0:T(1024)(128)(4,1)} %bitcast.19), calls=%async_computation.8 | async-start | bytes 8388608
  143.7 29.2 %slice-start.1 = ((s8[6291456]{0:T(1024)(128)(4,1)}), s8[2097152]{0:T(1024)(128)(4,1)S(1)}, s32[]{:S(2)}) async-start(s8[6291456]{0:T(1024)(128)(4,1)} %bitcast.19), calls=%async_computation.9 | async-start | bytes 4194304

commit v2 on v1

--- a/solution.py
+++ b/solution.py
@@ -161,6 +161,23 @@
 
 def per_device_fn(mesh):
     vmem = pl.BlockSpec(memory_space=pltpu.VMEM)
+    hbm = pl.BlockSpec(memory_space=pltpu.HBM)
+
+    def call(body, args, outs, copies=0, limit=8):
+        return pl.pallas_call(
+            body,
+            out_shape=outs,
+            in_specs=[spec for spec, _ in args],
+            out_specs=[vmem] * len(outs),
+            scratch_shapes=[pltpu.SemaphoreType.DMA((copies,))] if copies else [],
+            compiler_params=pltpu.CompilerParams(vmem_limit_bytes=limit << 20),
+        )(*[arg for _, arg in args])
+
+    def here(*arrays):
+        return [(vmem, x) for x in arrays]
+
+    def far(*arrays):
+        return [(hbm, pltpu.with_memory_space_constraint(x, pltpu.HBM)) for x in arrays]
 
     def run(latent, time_embedding, norm_gain, router, up_proj, down_proj, routes):
         tokens, width = latent.shape
@@ -173,51 +190,80 @@
         embedding = time_embedding.reshape(1, width)
         router_t = jnp.swapaxes(router, 1, 2)
         routes_t = jnp.swapaxes(routes, 2, 3)
-
-        def call(body, outs, args, **kw):
-            return pl.pallas_call(
-                body,
-                out_shape=outs,
-                in_specs=[vmem] * len(args),
-                out_specs=[vmem] * len(outs),
-                compiler_params=pltpu.CompilerParams(vmem_limit_bytes=16 << 20),
-                **kw,
-            )(*args)
-
-        state_shape = jax.ShapeDtypeStruct((tokens, width), f32)
+        up_t = jnp.swapaxes(up_proj, 2, 3)
+
+        out_shape = jax.ShapeDtypeStruct((tokens, width), f32)
+        state_shape = pltpu.VMEM((tokens, width), f32)
         slots_shape = pltpu.VMEM((plan.total, plan.piece), bf16)
         weight_shape = pltpu.VMEM((tokens, plan.total), f32)
-
-        def begin(step, layer):
-            def body(latent_ref, emb_ref, gain_ref, router_ref, routes_ref, state_ref, slots_ref, weight_ref):
+        up_shape = pltpu.VMEM((mine, hidden, width), bf16)
+
+        def own_experts(ref, layer):
+            base = lax.axis_index("mp") * mine if plan.share > 1 else 0
+            return ref.at[layer, pl.ds(base, mine)]
+
+        def begin():
+            inputs = [latent, embedding, norm_gain, router_t, routes_t]
+            count = len(inputs)
+
+            def body(*refs):
+                sources, (up_hbm,) = refs[:count], refs[count : count + 1]
+                copies = refs[count + 1 : 2 * count + 1]
+                state_ref, slots_ref, weight_ref, up_ref, sems = refs[2 * count + 1 :]
+                moves = [
+                    pltpu.make_async_copy(source, target, sems.at[i])
+                    for i, (source, target) in enumerate(zip(sources, copies))
+                ]
+                moves.append(pltpu.make_async_copy(own_experts(up_hbm, 0), up_ref, sems.at[count]))
+                for move in moves:
+                    move.start()
+                for move in moves[:count]:
+                    move.wait()
+                latent_ref, emb_ref, gain_ref, router_ref, routes_ref = copies
                 state = latent_ref[...] + start_time * emb_ref[...]
                 state_ref[...] = state
                 emit_dispatch(
-                    plan, state, gain_ref[layer : layer + 1], router_ref[layer],
-                    routes_ref[step, layer], slots_ref, weight_ref,
-                )
-
-            return call(
-                body, [state_shape, slots_shape, weight_shape],
-                [latent, embedding, norm_gain, router_t, routes_t],
+                    plan, state, gain_ref[0:1], router_ref[0], routes_ref[0, 0], slots_ref, weight_ref
+                )
+                moves[count].wait()
+
+            outs = call(
+                body,
+                far(*inputs, up_t),
+                [pltpu.VMEM(x.shape, x.dtype) for x in inputs]
+                + [state_shape, slots_shape, weight_shape, up_shape],
+                copies=count + 1,
             )
-
-        def middle(step, layer, state, weight, returned):
-            def body(state_in, weight_in, returned_ref, gain_ref, router_ref, routes_ref, state_ref, slots_ref, weight_ref):
+            return outs[:count], outs[count:]
+
+        def middle(small, step, layer, state, weight, returned, loading):
+            _, _, gain, router_s, routes_s = small
+
+            def body(state_in, weight_in, returned_ref, gain_ref, router_ref, routes_ref, *refs):
+                if loading:
+                    up_hbm, state_ref, slots_ref, weight_ref, up_ref, sems = refs
+                    move = pltpu.make_async_copy(own_experts(up_hbm, layer), up_ref, sems.at[0])
+                    move.start()
+                else:
+                    state_ref, slots_ref, weight_ref = refs
                 state = combine(plan, state_in[...], weight_in[...], returned_ref[...])
                 state_ref[...] = state
                 emit_dispatch(
                     plan, state, gain_ref[layer : layer + 1], router_ref[layer],
                     routes_ref[step, layer], slots_ref, weight_ref,
                 )
+                if loading:
+                    move.wait()
 
             return call(
-                body, [state_shape, slots_shape, weight_shape],
-                [state, weight, returned, norm_gain, router_t, routes_t],
+                body,
+                here(state, weight, returned, gain, router_s, routes_s) + (far(up_t) if loading else []),
+                [state_shape, slots_shape, weight_shape] + ([up_shape] if loading else []),
+                copies=int(loading),
             )
 
-        def turn(step, layer, state, weight, returned):
-            def body(latent_ref, emb_ref, state_in, weight_in, returned_ref, gain_ref, router_ref, routes_ref,
+        def turn(small, state, weight, returned):
+            def body(latent_ref, emb_ref, gain_ref, router_ref, routes_ref, state_in, weight_in, returned_ref,
                      first_ref, state_ref, slots_ref, weight_ref):
                 state = combine(plan, state_in[...], weight_in[...], returned_ref[...])
                 first = state - latent_ref[...]
@@ -226,16 +272,15 @@
                 state = moved + (start_time + step_size) * emb_ref[...]
                 state_ref[...] = state
                 emit_dispatch(
-                    plan, state, gain_ref[layer : layer + 1], router_ref[layer],
-                    routes_ref[step, layer], slots_ref, weight_ref,
+                    plan, state, gain_ref[0:1], router_ref[0], routes_ref[1, 0], slots_ref, weight_ref
                 )
 
             return call(
-                body, [state_shape, state_shape, slots_shape, weight_shape],
-                [latent, embedding, state, weight, returned, norm_gain, router_t, routes_t],
+                body, here(*small, state, weight, returned),
+                [state_shape, state_shape, slots_shape, weight_shape],
             )
 
-        def finish(state, weight, returned, first):
+        def finish(small, state, weight, returned, first):
             def body(latent_ref, state_in, weight_in, returned_ref, first_ref, next_ref, mean_ref):
                 state = combine(plan, state_in[...], weight_in[...], returned_ref[...])
                 first = first_ref[...]
@@ -244,87 +289,100 @@
                 mean_ref[...] = mean
                 next_ref[...] = latent_ref[...] + step_size * mean
 
-            return call(body, [state_shape, state_shape], [latent, state, weight, returned, first])
-
-        def load(layer):
-            def body(up_ref, down_ref, up_out, down_out, sems):
-                base = lax.axis_index("mp") * mine if plan.share > 1 else 0
-                a = pltpu.make_async_copy(up_ref.at[layer, pl.ds(base, mine)], up_out, sems.at[0])
-                b = pltpu.make_async_copy(down_ref.at[layer, pl.ds(base, mine)], down_out, sems.at[1])
-                a.start()
-                b.start()
-                a.wait()
-                b.wait()
-
-            return pl.pallas_call(
+            return call(body, here(small[0], state, weight, returned, first), [out_shape, out_shape])
+
+        each = plan.peers * CAP
+
+        def compute(arrived, up, down, layer):
+            loading = down is None
+
+            def body(arrived_ref, up_ref, down_in, out_ref, *refs):
+                if loading:
+                    down_ref, sems = refs
+                    move = pltpu.make_async_copy(own_experts(down_in, layer), down_ref, sems.at[0])
+                    move.start()
+                else:
+                    down_ref = down_in
+                total = plan.rows * plan.peers
+
+                def picks(shape, row_axis):
+                    row = lax.broadcasted_iota(i32, shape, row_axis)
+                    piece = lax.broadcasted_iota(i32, shape, 1 - row_axis)
+                    local = div(row, each)
+                    source = div(rem(row, each), CAP)
+                    target = source * plan.block + local * CAP + rem(row, CAP)
+                    return [
+                        jnp.where(piece == target + p * plan.rows, 1.0, 0.0).astype(bf16)
+                        for p in range(plan.parts)
+                    ]
+
+                arrived = arrived_ref[...]
+                rows = jnp.concatenate(
+                    [
+                        jnp.dot(pick, arrived, preferred_element_type=f32).astype(bf16)
+                        for pick in picks((total, plan.total), 0)
+                    ],
+                    axis=1,
+                )
+                hids = [
+                    jax.nn.gelu(
+                        lax.dot_general(
+                            rows[local * each : (local + 1) * each],
+                            up_ref[local],
+                            (((1,), (1,)), ((), ())),
+                            preferred_element_type=f32,
+                        ),
+                        approximate=True,
+                    ).astype(bf16)
+                    for local in range(mine)
+                ]
+                if loading:
+                    move.wait()
+                result = jnp.concatenate(
+                    [
+                        jnp.dot(hids[local], down_ref[local], preferred_element_type=f32).astype(bf16)
+                        for local in range(mine)
+                    ],
+                    axis=0,
+                )
+                out = jnp.zeros((plan.total, plan.piece), f32)
+                for p, pick in enumerate(picks((plan.total, total), 1)):
+                    out = out + jnp.dot(
+                        pick, result[:, p * plan.piece : (p + 1) * plan.piece], preferred_element_type=f32
+                    )
+                out_ref[...] = out.astype(bf16)
+
+            down_args = far(down_proj) if loading else here(down)
+            outs = call(
                 body,
-                out_shape=[
-                    pltpu.VMEM((mine, width, hidden), bf16),
-                    pltpu.VMEM((mine, hidden, width), bf16),
-                ],
-                in_specs=[pl.BlockSpec(memory_space=pl.ANY)] * 2,
-                out_specs=[vmem] * 2,
-                scratch_shapes=[pltpu.SemaphoreType.DMA((2,))],
-                compiler_params=pltpu.CompilerParams(vmem_limit_bytes=2 << 20),
-            )(up_proj, down_proj)
-
-        each = plan.peers * CAP
-
-        def experts_body(arrived_ref, up_ref, down_ref, out_ref):
-            total = plan.rows * plan.peers
-
-            def picks(shape, row_axis):
-                row = lax.broadcasted_iota(i32, shape, row_axis)
-                piece = lax.broadcasted_iota(i32, shape, 1 - row_axis)
-                local = div(row, each)
-                source = div(rem(row, each), CAP)
-                target = source * plan.block + local * CAP + rem(row, CAP)
-                return [
-                    jnp.where(piece == target + p * plan.rows, 1.0, 0.0).astype(bf16)
-                    for p in range(plan.parts)
-                ]
-
-            arrived = arrived_ref[...]
-            rows = jnp.concatenate(
-                [
-                    jnp.dot(pick, arrived, preferred_element_type=f32).astype(bf16)
-                    for pick in picks((total, plan.total), 0)
-                ],
-                axis=1,
+                here(arrived, up) + down_args,
+                [slots_shape] + ([pltpu.VMEM((mine, hidden, width), bf16)] if loading else []),
+                copies=int(loading),
+                limit=16,
             )
-            results = []
-            for local in range(mine):
-                own = rows[local * each : (local + 1) * each]
-                hid = jax.nn.gelu(
-                    jnp.dot(own, up_ref[local], preferred_element_type=f32), approximate=True
-                ).astype(bf16)
-                results.append(jnp.dot(hid, down_ref[local], preferred_element_type=f32).astype(bf16))
-            result = jnp.concatenate(results, axis=0)
-            out = jnp.zeros((plan.total, plan.piece), f32)
-            for p, pick in enumerate(picks((plan.total, total), 1)):
-                out = out + jnp.dot(
-                    pick, result[:, p * plan.piece : (p + 1) * plan.piece], preferred_element_type=f32
-                )
-            out_ref[...] = out.astype(bf16)
-
-        def compute(arrived, layer_weights):
-            return call(experts_body, [slots_shape], [arrived, *layer_weights])[0]
+            return outs[0], (outs[1] if loading else down)
 
         def exchange(x):
             return lax.all_to_all(x, plan.axes, split_axis=0, concat_axis=0, tiled=True)
 
-        state, slots, weight = begin(0, 0)
-        loaded = [load(layer) for layer in range(layers)]
-        first = None
+        small, (state, slots, weight, up) = begin()
+        ups, downs, first = [up], [], None
         for step in range(2):
             for layer in range(layers):
-                returned = exchange(compute(exchange(slots), loaded[layer]))
+                result, down = compute(
+                    exchange(slots), ups[layer], downs[layer] if step else None, layer
+                )
+                downs.append(down)
+                returned = exchange(result)
                 if layer + 1 < layers:
-                    state, slots, weight = middle(step, layer + 1, state, weight, returned)
+                    state, slots, weight, *loaded = middle(
+                        small, step, layer + 1, state, weight, returned, step == 0
+                    )
+                    ups.extend(loaded)
                 elif step == 0:
-                    first, state, slots, weight = turn(1, 0, state, weight, returned)
+                    first, state, slots, weight = turn(small, state, weight, returned)
                 else:
-                    return tuple(finish(state, weight, returned, first))
+                    return tuple(finish(small, state, weight, returned, first))
 
     return run
 

time: 191 us -> 134 us (0.70)
  local copies, waits for them, and re-layouts: 72.3 us -> 0 us
  blocking collectives: 82.8 us -> 106 us
  starting transfers between devices: 10.9 us -> 0 us
  Pallas kernels: 22.6 us -> 26.6 us
    unnamed x49 -> x0, local copies, waits for them, and re-layouts: 72.3 us -> none
    all_to_all x6 -> x8, blocking collectives: 82.8 us -> 106 us  [exchange(): return lax.all_to_all(x, plan.axes, split_axis=0, concat_axis=0, tiled=True)]
    all_to_all x2 -> x0, starting transfers between devices: 10.9 us -> none  [exchange(): return lax.all_to_all(x, plan.axes, split_axis=0, concat_axis=0, tiled=True)]
    pallas_call x11 -> x9, Pallas kernels: 22.6 us -> 26.6 us  [call(): pl.pallas_call(body, out_shape=outs, in_specs=[spec for spec, _ in args],...]
  transfers between devices with their start and end apart: 2 -> 0, of which waited for: 0 -> 0; matrix products, arithmetic and copies ran while one was open for 17% -> 0% of each run, Pallas kernels for 3% -> 0%
where the time goes in v2:
time: 134 us; the launch traced here: 133 us
  blocking collectives  106 us (79%)
  Pallas kernels  26.6 us (20%)
    all_to_all x8, blocking collectives, exchange(): return lax.all_to_all(x, plan.axes, split_axis=0, concat_axis=0, tiled=True)  106 us
    pallas_call x9, Pallas kernels, call(): pl.pallas_call(body, out_shape=outs, in_specs=[spec for spec, _ in args],...  26.6 us

profile of v2, /device:TPU:0, one launch (start us, length us, event | category | flops | bytes accessed | tf_op | source)
XLA Modules:
  0.0 133.4 jit_solution(10295289045715315680)
XLA Ops:
  0.6 2.9 %shard_map.86 = (f32[16,2048]{1,0:T(8,128)S(1)}, f32[1,2048]{1,0:T(1,128)S(1)}, f32[2,2048]{1,0:T(2,128)S(1)}, f32[2,16,2048]{2,1,0:T(8,128)S(1)}, s32[2,2,2,16]...) custom-call(f32[16,2048]{1,0:T(8,128)} %refs_0_.1, ...), custom_call_target="tpu_custom_call" | custom-call | tf_op jit(solution)/shard_map/pallas_call | solution.py:167
  3.5 17.2 %all_to_all.88 = bf16[16,8,1024]{2,1,0:T(8,128)(2,1)S(1)} all-to-all(bf16[16,8,1024]{2,1,0:T(8,128)(2,1)S(1)} %bitcast.30), channel_id=1, replica_groups=mesh['groups'=2,'expert'=4,'dp'=2,'mp'=2] {'expert','dp','mp'}, dimensions={0} | all-to-all | bytes 524288 | tf_op jit(solution)/shard_map/all_to_all | solution.py:366
  20.7 5.7 %shard_map.87 = (bf16[128,1024]{1,0:T(8,128)(2,1)S(1)}, bf16[2,704,2048]{2,1,0:T(8,128)(2,1)S(1)}) custom-call(bf16[128,1024]{1,0:T(8,128)(2,1)S(1)} %bitcast.21, bf16[2,704,2048]{2,1,0:T(8,128)(2,1)S(1)} %get-tuple-element.34.up_ref, bf16[2,4,704,2048]{3,2,1,0:T(8,128)(2,1)} %down_in.3), custom_call_target="tpu_custom_call" | custom-call | tf_op jit(solution)/shard_map/pallas_call | solution.py:167
  26.4 12.7 %all_to_all.89 = bf16[16,8,1024]{2,1,0:T(8,128)(2,1)S(1)} all-to-all(bf16[16,8,1024]{2,1,0:T(8,128)(2,1)S(1)} %bitcast.34), channel_id=1, replica_groups=mesh['groups'=2,'expert'=4,'dp'=2,'mp'=2] {'expert','dp','mp'}, dimensions={0} | all-to-all | bytes 524288 | tf_op jit(solution)/shard_map/all_to_all | solution.py:366
  39.1 3.4 %shard_map.88 = (f32[16,2048]{1,0:T(8,128)S(1)}, bf16[128,1024]{1,0:T(8,128)(2,1)S(1)}, f32[16,128]{1,0:T(8,128)S(1)}, bf16[2,704,2048]{2,1,0:T(8,128)(2,1)S(1)}) custom-call(f32[16,2048]{1,0:T(8,128)S(1)} %get-tuple-element.31.state_in, f32[16,128]{1,0:T(8,128)S(1)} %get-tuple-element.32.weight_in, bf16[128,1024]{1,0:T(8,128)(2,1)S(1)} %bitcast.20, ...), custom_call_target="tpu_custom_call" | custom-call | tf_op jit(solution)/shard_map/pallas_call | solution.py:167
  42.5 12.7 %all_to_all.90 = bf16[16,8,1024]{2,1,0:T(8,128)(2,1)S(1)} all-to-all(bf16[16,8,1024]{2,1,0:T(8,128)(2,1)S(1)} %bitcast.33), channel_id=1, replica_groups=mesh['groups'=2,'expert'=4,'dp'=2,'mp'=2] {'expert','dp','mp'}, dimensions={0} | all-to-all | bytes 524288 | tf_op jit(solution)/shard_map/all_to_all | solution.py:366
  55.2 5.7 %shard_map.89 = (bf16[128,1024]{1,0:T(8,128)(2,1)S(1)}, bf16[2,704,2048]{2,1,0:T(8,128)(2,1)S(1)}) custom-call(bf16[128,1024]{1,0:T(8,128)(2,1)S(1)} %bitcast.22, bf16[2,704,2048]{2,1,0:T(8,128)(2,1)S(1)} %get-tuple-element.39.up_ref, bf16[2,4,704,2048]{3,2,1,0:T(8,128)(2,1)} %down_in.3), custom_call_target="tpu_custom_call" | custom-call | tf_op jit(solution)/shard_map/pallas_call | solution.py:167
  60.9 12.7 %all_to_all.91 = bf16[16,8,1024]{2,1,0:T(8,128)(2,1)S(1)} all-to-all(bf16[16,8,1024]{2,1,0:T(8,128)(2,1)S(1)} %bitcast.35), channel_id=1, replica_groups=mesh['groups'=2,'expert'=4,'dp'=2,'mp'=2] {'expert','dp','mp'}, dimensions={0} | all-to-all | bytes 524288 | tf_op jit(solution)/shard_map/all_to_all | solution.py:366
  73.6 0.9 shard_map.90
  74.6 12.7 %all_to_all.92 = bf16[16,8,1024]{2,1,0:T(8,128)(2,1)S(1)} all-to-all(bf16[16,8,1024]{2,1,0:T(8,128)(2,1)S(1)} %bitcast.32), channel_id=1, replica_groups=mesh['groups'=2,'expert'=4,'dp'=2,'mp'=2] {'expert','dp','mp'}, dimensions={0} | all-to-all | bytes 524288 | tf_op jit(solution)/shard_map/all_to_all | solution.py:366
  87.3 3.1 %shard_map.91 = bf16[128,1024]{1,0:T(8,128)(2,1)S(1)} custom-call(bf16[128,1024]{1,0:T(8,128)(2,1)S(1)} %bitcast.24, bf16[2,704,2048]{2,1,0:T(8,128)(2,1)S(1)} %get-tuple-element.34.up_ref, bf16[2,704,2048]{2,1,0:T(8,128)(2,1)S(1)} %get-tuple-element.44.down_in), custom_call_target="tpu_custom_call" | custom-call | tf_op jit(solution)/shard_map/pallas_call | solution.py:167
  90.4 12.7 %all_to_all.93 = bf16[16,8,1024]{2,1,0:T(8,128)(2,1)S(1)} all-to-all(bf16[16,8,1024]{2,1,0:T(8,128)(2,1)S(1)} %bitcast.26), channel_id=1, replica_groups=mesh['groups'=2,'expert'=4,'dp'=2,'mp'=2] {'expert','dp','mp'}, dimensions={0} | all-to-all | bytes 524288 | tf_op jit(solution)/shard_map/all_to_all | solution.py:366
  103.0 0.9 shard_map.92
  104.0 12.7 %all_to_all.94 = bf16[16,8,1024]{2,1,0:T(8,128)(2,1)S(1)} all-to-all(bf16[16,8,1024]{2,1,0:T(8,128)(2,1)S(1)} %bitcast.31), channel_id=1, replica_groups=mesh['groups'=2,'expert'=4,'dp'=2,'mp'=2] {'expert','dp','mp'}, dimensions={0} | all-to-all | bytes 524288 | tf_op jit(solution)/shard_map/all_to_all | solution.py:366
  116.7 3.1 %shard_map.93 = bf16[128,1024]{1,0:T(8,128)(2,1)S(1)} custom-call(bf16[128,1024]{1,0:T(8,128)(2,1)S(1)} %bitcast.25, bf16[2,704,2048]{2,1,0:T(8,128)(2,1)S(1)} %get-tuple-element.39.up_ref, bf16[2,704,2048]{2,1,0:T(8,128)(2,1)S(1)} %get-tuple-element.48.down_in), custom_call_target="tpu_custom_call" | custom-call | tf_op jit(solution)/shard_map/pallas_call | solution.py:167
  119.8 12.7 %all_to_all.95 = bf16[16,8,1024]{2,1,0:T(8,128)(2,1)S(1)} all-to-all(bf16[16,8,1024]{2,1,0:T(8,128)(2,1)S(1)} %bitcast.27), channel_id=1, replica_groups=mesh['groups'=2,'expert'=4,'dp'=2,'mp'=2] {'expert','dp','mp'}, dimensions={0} | all-to-all | bytes 524288 | tf_op jit(solution)/shard_map/all_to_all | solution.py:366
  132.5 0.9 shard_map.94

commit v3 on v2

--- a/solution.py
+++ b/solution.py
@@ -163,7 +163,7 @@
     vmem = pl.BlockSpec(memory_space=pltpu.VMEM)
     hbm = pl.BlockSpec(memory_space=pltpu.HBM)
 
-    def call(body, args, outs, copies=0, limit=8):
+    def call(body, args, outs, copies=0, limit=4):
         return pl.pallas_call(
             body,
             out_shape=outs,
@@ -171,6 +171,7 @@
             out_specs=[vmem] * len(outs),
             scratch_shapes=[pltpu.SemaphoreType.DMA((copies,))] if copies else [],
             compiler_params=pltpu.CompilerParams(vmem_limit_bytes=limit << 20),
+            cost_estimate=pl.CostEstimate(flops=10**11, transcendentals=0, bytes_accessed=10**9),
         )(*[arg for _, arg in args])
 
     def here(*arrays):
@@ -196,28 +197,21 @@
         state_shape = pltpu.VMEM((tokens, width), f32)
         slots_shape = pltpu.VMEM((plan.total, plan.piece), bf16)
         weight_shape = pltpu.VMEM((tokens, plan.total), f32)
-        up_shape = pltpu.VMEM((mine, hidden, width), bf16)
-
-        def own_experts(ref, layer):
-            base = lax.axis_index("mp") * mine if plan.share > 1 else 0
-            return ref.at[layer, pl.ds(base, mine)]
 
         def begin():
             inputs = [latent, embedding, norm_gain, router_t, routes_t]
             count = len(inputs)
 
             def body(*refs):
-                sources, (up_hbm,) = refs[:count], refs[count : count + 1]
-                copies = refs[count + 1 : 2 * count + 1]
-                state_ref, slots_ref, weight_ref, up_ref, sems = refs[2 * count + 1 :]
+                sources, copies = refs[:count], refs[count : 2 * count]
+                state_ref, slots_ref, weight_ref, sems = refs[2 * count :]
                 moves = [
                     pltpu.make_async_copy(source, target, sems.at[i])
                     for i, (source, target) in enumerate(zip(sources, copies))
                 ]
-                moves.append(pltpu.make_async_copy(own_experts(up_hbm, 0), up_ref, sems.at[count]))
                 for move in moves:
                     move.start()
-                for move in moves[:count]:
+                for move in moves:
                     move.wait()
                 latent_ref, emb_ref, gain_ref, router_ref, routes_ref = copies
                 state = latent_ref[...] + start_time * emb_ref[...]
@@ -225,41 +219,27 @@
                 emit_dispatch(
                     plan, state, gain_ref[0:1], router_ref[0], routes_ref[0, 0], slots_ref, weight_ref
                 )
-                moves[count].wait()
 
             outs = call(
                 body,
-                far(*inputs, up_t),
-                [pltpu.VMEM(x.shape, x.dtype) for x in inputs]
-                + [state_shape, slots_shape, weight_shape, up_shape],
-                copies=count + 1,
+                far(*inputs),
+                [pltpu.VMEM(x.shape, x.dtype) for x in inputs] + [state_shape, slots_shape, weight_shape],
+                copies=count,
             )
             return outs[:count], outs[count:]
 
-        def middle(small, step, layer, state, weight, returned, loading):
-            _, _, gain, router_s, routes_s = small
-
-            def body(state_in, weight_in, returned_ref, gain_ref, router_ref, routes_ref, *refs):
-                if loading:
-                    up_hbm, state_ref, slots_ref, weight_ref, up_ref, sems = refs
-                    move = pltpu.make_async_copy(own_experts(up_hbm, layer), up_ref, sems.at[0])
-                    move.start()
-                else:
-                    state_ref, slots_ref, weight_ref = refs
+        def middle(small, step, layer, state, weight, returned):
+            def body(gain_ref, router_ref, routes_ref, state_in, weight_in, returned_ref,
+                     state_ref, slots_ref, weight_ref):
                 state = combine(plan, state_in[...], weight_in[...], returned_ref[...])
                 state_ref[...] = state
                 emit_dispatch(
                     plan, state, gain_ref[layer : layer + 1], router_ref[layer],
                     routes_ref[step, layer], slots_ref, weight_ref,
                 )
-                if loading:
-                    move.wait()
 
             return call(
-                body,
-                here(state, weight, returned, gain, router_s, routes_s) + (far(up_t) if loading else []),
-                [state_shape, slots_shape, weight_shape] + ([up_shape] if loading else []),
-                copies=int(loading),
+                body, here(*small[2:], state, weight, returned), [state_shape, slots_shape, weight_shape]
             )
 
         def turn(small, state, weight, returned):
@@ -293,16 +273,9 @@
 
         each = plan.peers * CAP
 
-        def compute(arrived, up, down, layer):
-            loading = down is None
-
-            def body(arrived_ref, up_ref, down_in, out_ref, *refs):
-                if loading:
-                    down_ref, sems = refs
-                    move = pltpu.make_async_copy(own_experts(down_in, layer), down_ref, sems.at[0])
-                    move.start()
-                else:
-                    down_ref = down_in
+        def compute(arrived, layer):
+            def body(arrived_ref, up_ref, down_ref, out_ref):
+                base = lax.axis_index("mp") * mine if plan.share > 1 else 0
                 total = plan.rows * plan.peers
 
                 def picks(shape, row_axis):
@@ -324,27 +297,21 @@
                     ],
                     axis=1,
                 )
-                hids = [
-                    jax.nn.gelu(
+                results = []
+                for local in range(mine):
+                    hid = jax.nn.gelu(
                         lax.dot_general(
                             rows[local * each : (local + 1) * each],
-                            up_ref[local],
+                            up_ref[layer, base + local],
                             (((1,), (1,)), ((), ())),
                             preferred_element_type=f32,
                         ),
                         approximate=True,
                     ).astype(bf16)
-                    for local in range(mine)
-                ]
-                if loading:
-                    move.wait()
-                result = jnp.concatenate(
-                    [
-                        jnp.dot(hids[local], down_ref[local], preferred_element_type=f32).astype(bf16)
-                        for local in range(mine)
-                    ],
-                    axis=0,
-                )
+                    results.append(
+                        jnp.dot(hid, down_ref[layer, base + local], preferred_element_type=f32).astype(bf16)
+                    )
+                result = jnp.concatenate(results, axis=0)
                 out = jnp.zeros((plan.total, plan.piece), f32)
                 for p, pick in enumerate(picks((plan.total, total), 1)):
                     out = out + jnp.dot(
@@ -352,33 +319,17 @@
                     )
                 out_ref[...] = out.astype(bf16)
 
-            down_args = far(down_proj) if loading else here(down)
-            outs = call(
-                body,
-                here(arrived, up) + down_args,
-                [slots_shape] + ([pltpu.VMEM((mine, hidden, width), bf16)] if loading else []),
-                copies=int(loading),
-                limit=16,
-            )
-            return outs[0], (outs[1] if loading else down)
+            return call(body, here(arrived, up_t, down_proj), [slots_shape], limit=6)[0]
 
         def exchange(x):
             return lax.all_to_all(x, plan.axes, split_axis=0, concat_axis=0, tiled=True)
 
-        small, (state, slots, weight, up) = begin()
-        ups, downs, first = [up], [], None
+        small, (state, slots, weight) = begin()
         for step in range(2):
             for layer in range(layers):
-                result, down = compute(
-                    exchange(slots), ups[layer], downs[layer] if step else None, layer
-                )
-                downs.append(down)
-                returned = exchange(result)
+                returned = exchange(compute(exchange(slots), layer))
                 if layer + 1 < layers:
-                    state, slots, weight, *loaded = middle(
-                        small, step, layer + 1, state, weight, returned, step == 0
-                    )
-                    ups.extend(loaded)
+                    state, slots, weight = middle(small, step, layer + 1, state, weight, returned)
                 elif step == 0:
                     first, state, slots, weight = turn(small, state, weight, returned)
                 else:

time: 134 us -> 129 us (0.963)
  Pallas kernels: 26.6 us -> 20.7 us
    pallas_call x9, Pallas kernels: 26.6 us -> 20.7 us  [call(): pl.pallas_call(body, out_shape=outs, in_specs=[spec for spec, _ in args],...]
where the time goes in v3:
time: 129 us; the launch traced here: 128 us
  blocking collectives  107 us (83%)
  Pallas kernels  20.7 us (16%)
    all_to_all x8, blocking collectives, exchange(): return lax.all_to_all(x, plan.axes, split_axis=0, concat_axis=0, tiled=True)  107 us
    pallas_call x9, Pallas kernels, call(): pl.pallas_call(body, out_shape=outs, in_specs=[spec for spec, _ in args],...  20.7 us

profile of v3, /device:TPU:0, one launch (start us, length us, event | category | flops | bytes accessed | tf_op | source)
XLA Modules:
  0.0 128.2 jit_solution(4898928893354140524)
XLA Ops:
  0.6 0.0 copy-start
  0.6 0.0 copy-start.2
  0.7 2.0 %shard_map.86 = (f32[16,2048]{1,0:T(8,128)S(1)}, f32[1,2048]{1,0:T(1,128)S(1)}, f32[2,2048]{1,0:T(2,128)S(1)}, f32[2,16,2048]{2,1,0:T(8,128)S(1)}, s32[2,2,2,16]...) custom-call(f32[16,2048]{1,0:T(8,128)} %refs_0_.1, ...), custom_call_target="tpu_custom_call" | custom-call | flops 99999997952 | bytes 1000000000 | tf_op jit(solution)/shard_map/pallas_call | solution.py:167
  2.6 17.5 %all_to_all.88 = bf16[16,8,1024]{2,1,0:T(8,128)(2,1)S(1)} all-to-all(bf16[16,8,1024]{2,1,0:T(8,128)(2,1)S(1)} %bitcast.24), channel_id=1, replica_groups=mesh['groups'=2,'expert'=4,'dp'=2,'mp'=2] {'expert','dp','mp'}, dimensions={0} | all-to-all | bytes 524288 | tf_op jit(solution)/shard_map/all_to_all | solution.py:325
  20.1 0.0 copy-done
  20.1 0.0 copy-done.2
  20.1 3.7 %shard_map.87 = bf16[128,1024]{1,0:T(8,128)(2,1)S(1)} custom-call(bf16[128,1024]{1,0:T(8,128)(2,1)S(1)} %bitcast.28, bf16[2,4,704,2048]{3,2,1,0:T(8,128)(2,1)S(1)} %bitcast.36, bf16[2,4,704,2048]{3,2,1,0:T(8,128)(2,1)S(1)} %copy-done.2), custom_call_target="tpu_custom_call" | custom-call | flops 99999997952 | bytes 1000000000 | tf_op jit(solution)/shard_map/pallas_call | solution.py:167
  23.9 12.7 %all_to_all.89 = bf16[16,8,1024]{2,1,0:T(8,128)(2,1)S(1)} all-to-all(bf16[16,8,1024]{2,1,0:T(8,128)(2,1)S(1)} %bitcast.29), channel_id=1, replica_groups=mesh['groups'=2,'expert'=4,'dp'=2,'mp'=2] {'expert','dp','mp'}, dimensions={0} | all-to-all | bytes 524288 | tf_op jit(solution)/shard_map/all_to_all | solution.py:325
  36.5 0.0 copy-start.1
  36.6 0.0 copy-start.3
  36.6 0.9 shard_map.88
  37.5 13.1 %all_to_all.90 = bf16[16,8,1024]{2,1,0:T(8,128)(2,1)S(1)} all-to-all(bf16[16,8,1024]{2,1,0:T(8,128)(2,1)S(1)} %bitcast.27), channel_id=1, replica_groups=mesh['groups'=2,'expert'=4,'dp'=2,'mp'=2] {'expert','dp','mp'}, dimensions={0} | all-to-all | bytes 524288 | tf_op jit(solution)/shard_map/all_to_all | solution.py:325
  50.6 0.0 copy-done.1
  50.6 0.0 copy-done.3
  50.7 3.7 %shard_map.89 = bf16[128,1024]{1,0:T(8,128)(2,1)S(1)} custom-call(bf16[128,1024]{1,0:T(8,128)(2,1)S(1)} %bitcast.30, bf16[2,4,704,2048]{3,2,1,0:T(8,128)(2,1)S(1)} %bitcast.37, bf16[2,4,704,2048]{3,2,1,0:T(8,128)(2,1)S(1)} %copy-done.3), custom_call_target="tpu_custom_call" | custom-call | flops 99999997952 | bytes 1000000000 | tf_op jit(solution)/shard_map/pallas_call | solution.py:167
  54.4 12.7 %all_to_all.91 = bf16[16,8,1024]{2,1,0:T(8,128)(2,1)S(1)} all-to-all(bf16[16,8,1024]{2,1,0:T(8,128)(2,1)S(1)} %bitcast.31), channel_id=1, replica_groups=mesh['groups'=2,'expert'=4,'dp'=2,'mp'=2] {'expert','dp','mp'}, dimensions={0} | all-to-all | bytes 524288 | tf_op jit(solution)/shard_map/all_to_all | solution.py:325
  67.1 0.9 shard_map.90
  68.1 12.7 %all_to_all.92 = bf16[16,8,1024]{2,1,0:T(8,128)(2,1)S(1)} all-to-all(bf16[16,8,1024]{2,1,0:T(8,128)(2,1)S(1)} %bitcast.25), channel_id=1, replica_groups=mesh['groups'=2,'expert'=4,'dp'=2,'mp'=2] {'expert','dp','mp'}, dimensions={0} | all-to-all | bytes 524288 | tf_op jit(solution)/shard_map/all_to_all | solution.py:325
  80.7 3.7 %shard_map.91 = bf16[128,1024]{1,0:T(8,128)(2,1)S(1)} custom-call(bf16[128,1024]{1,0:T(8,128)(2,1)S(1)} %bitcast.32, bf16[2,4,704,2048]{3,2,1,0:T(8,128)(2,1)S(1)} %bitcast.38, bf16[2,4,704,2048]{3,2,1,0:T(8,128)(2,1)S(1)} %copy-done.3), custom_call_target="tpu_custom_call" | custom-call | flops 99999997952 | bytes 1000000000 | tf_op jit(solution)/shard_map/pallas_call | solution.py:167
  84.5 12.7 %all_to_all.93 = bf16[16,8,1024]{2,1,0:T(8,128)(2,1)S(1)} all-to-all(bf16[16,8,1024]{2,1,0:T(8,128)(2,1)S(1)} %bitcast.33), channel_id=1, replica_groups=mesh['groups'=2,'expert'=4,'dp'=2,'mp'=2] {'expert','dp','mp'}, dimensions={0} | all-to-all | bytes 524288 | tf_op jit(solution)/shard_map/all_to_all | solution.py:325
  97.2 0.9 shard_map.92
  98.1 12.7 %all_to_all.94 = bf16[16,8,1024]{2,1,0:T(8,128)(2,1)S(1)} all-to-all(bf16[16,8,1024]{2,1,0:T(8,128)(2,1)S(1)} %bitcast.22), channel_id=1, replica_groups=mesh['groups'=2,'expert'=4,'dp'=2,'mp'=2] {'expert','dp','mp'}, dimensions={0} | all-to-all | bytes 524288 | tf_op jit(solution)/shard_map/all_to_all | solution.py:325
  110.8 3.7 %shard_map.93 = bf16[128,1024]{1,0:T(8,128)(2,1)S(1)} custom-call(bf16[128,1024]{1,0:T(8,128)(2,1)S(1)} %bitcast.34, bf16[2,4,704,2048]{3,2,1,0:T(8,128)(2,1)S(1)} %bitcast.39, bf16[2,4,704,2048]{3,2,1,0:T(8,128)(2,1)S(1)} %copy-done.3), custom_call_target="tpu_custom_call" | custom-call | flops 99999997952 | bytes 1000000000 | tf_op jit(solution)/shard_map/pallas_call | solution.py:167
  114.5 12.8 %all_to_all.95 = bf16[16,8,1024]{2,1,0:T(8,128)(2,1)S(1)} all-to-all(bf16[16,8,1024]{2,1,0:T(8,128)(2,1)S(1)} %bitcast.35), channel_id=1, replica_groups=mesh['groups'=2,'expert'=4,'dp'=2,'mp'=2] {'expert','dp','mp'}, dimensions={0} | all-to-all | bytes 524288 | tf_op jit(solution)/shard_map/all_to_all | solution.py:325
  127.3 0.9 shard_map.94
Async XLA Ops:
  0.6 19.5 %copy-start = (bf16[2,4,2048,704]{2,3,1,0:T(8,128)(2,1)S(1)}, bf16[2,4,2048,704]{2,3,1,0:T(8,128)(2,1)}, u32[]{:S(2)}) copy-start(bf16[2,4,2048,704]{2,3,1,0:T(8,128)(2,1)} %param.11) | copy-start | bytes 69206016
  0.6 19.5 %copy-start.2 = (bf16[2,4,704,2048]{3,2,1,0:T(8,128)(2,1)S(1)}, bf16[2,4,704,2048]{3,2,1,0:T(8,128)(2,1)}, u32[]{:S(2)}) copy-start(bf16[2,4,704,2048]{3,2,1,0:T(8,128)(2,1)} %down_ref.7) | copy-start | bytes 69206016
  36.5 14.1 %copy-start.1 = (bf16[2,4,2048,704]{2,3,1,0:T(8,128)(2,1)S(1)}, bf16[2,4,2048,704]{2,3,1,0:T(8,128)(2,1)}, u32[]{:S(2)}) copy-start(bf16[2,4,2048,704]{2,3,1,0:T(8,128)(2,1)} %param.11) | copy-start | bytes 69206016
  36.6 14.1 %copy-start.3 = (bf16[2,4,704,2048]{3,2,1,0:T(8,128)(2,1)S(1)}, bf16[2,4,704,2048]{3,2,1,0:T(8,128)(2,1)}, u32[]{:S(2)}) copy-start(bf16[2,4,704,2048]{3,2,1,0:T(8,128)(2,1)} %down_ref.7) | copy-start | bytes 69206016

commit v4 on v3

--- a/solution.py
+++ b/solution.py
@@ -32,30 +32,42 @@
 
 class Plan:
     def __init__(self, mesh, tokens, width, experts, local_experts):
-        n_mp = mesh.shape["mp"]
-        self.share = n_mp if local_experts % n_mp == 0 else 1
-        self.axes = ("expert", "dp", "mp") if self.share > 1 else ("expert", "dp")
-        self.n_dp = mesh.shape["dp"]
-        self.peers = mesh.shape["expert"] * self.n_dp * self.share
+        for shares in (("groups", "mp"), ("mp",), ()):
+            share = math.prod(mesh.shape[axis] for axis in shares)
+            if local_experts % share == 0:
+                break
+        self.shares = shares
+        self.mine = local_experts // share
+        self.axes = tuple(a for a in ("groups", "expert", "dp", "mp") if a in ("expert", "dp") + shares)
+        self.sizes = [mesh.shape[axis] for axis in self.axes]
+        self.peers = math.prod(self.sizes)
         self.tokens = tokens
         self.width = width
         self.experts = experts
         self.local_experts = local_experts
-        self.mine = local_experts // self.share
         self.rows = self.mine * CAP
         self.parts = 8 // math.gcd(8, self.rows)
         self.piece = width // self.parts
         self.block = self.rows * self.parts
         self.total = self.peers * self.block
 
+    def first_expert(self, place):
+        share = 0
+        for axis in self.shares:
+            size = self.sizes[self.axes.index(axis)]
+            share = share * size + place[axis]
+        return share * self.mine
+
     def where(self, index):
         peer = div(index, self.block)
         inner = rem(index, self.block)
         part = div(inner, self.rows)
         row = rem(inner, self.rows)
-        expert = div(peer, self.n_dp * self.share) * self.local_experts
-        if self.share > 1:
-            expert = expert + rem(peer, self.share) * self.mine
+        place = {}
+        for axis, size in reversed(list(zip(self.axes, self.sizes))):
+            place[axis] = rem(peer, size)
+            peer = div(peer, size)
+        expert = place["expert"] * self.local_experts + self.first_expert(place)
         return part, expert + div(row, CAP), rem(row, CAP)
 
 
@@ -66,36 +78,10 @@
     return jnp.sum(jnp.where(eye, row, 0), axis=1, keepdims=True)
 
 
-def dispatch_select(plan, first, second):
-    shape = (plan.total, plan.tokens)
-    part, expert, slot = plan.where(lax.broadcasted_iota(i32, shape, 0))
-    named = jnp.where((first == expert) | (second == expert), 1.0, 0.0)
-    earlier = jnp.where(
-        lax.broadcasted_iota(i32, (plan.tokens, plan.tokens), 0)
-        < lax.broadcasted_iota(i32, (plan.tokens, plan.tokens), 1),
-        1.0,
-        0.0,
+def by_part(plan, part, terms):
+    return jnp.concatenate(
+        [jnp.where(part == p, term, 0.0) for p in range(plan.parts) for term in terms], axis=0
     ).astype(bf16)
-    before = jnp.dot(named.astype(bf16), earlier, preferred_element_type=f32)
-    chosen = jnp.where(before == slot.astype(f32), named, 0.0)
-    return [jnp.where(part == p, chosen, 0.0).astype(bf16) for p in range(plan.parts)]
-
-
-def combine_select(plan, first, second, mix):
-    shape = (plan.tokens, plan.total)
-    part, expert, slot = plan.where(lax.broadcasted_iota(i32, shape, 1))
-    is_first = first == expert
-    is_second = second == expert
-    named = jnp.where(is_first | is_second, 1.0, 0.0)
-    earlier = jnp.where(
-        lax.broadcasted_iota(i32, (plan.tokens, plan.tokens), 1)
-        < lax.broadcasted_iota(i32, (plan.tokens, plan.tokens), 0),
-        1.0,
-        0.0,
-    ).astype(bf16)
-    before = jnp.dot(earlier, named.astype(bf16), preferred_element_type=f32)
-    weight = jnp.where(is_first, mix, 0.0) + jnp.where(is_second, 1.0 - mix, 0.0)
-    return jnp.where(before == slot.astype(f32), weight, 0.0)
 
 
 def combine(plan, state, weight, returned):
@@ -103,15 +89,9 @@
     high = weight.astype(bf16).astype(f32)
     middle = (weight - high).astype(bf16).astype(f32)
     low = weight - high - middle
-    stacked = jnp.concatenate(
-        [
-            jnp.where(part == p, term, 0.0)
-            for p in range(plan.parts)
-            for term in (high, middle, low)
-        ],
-        axis=0,
-    ).astype(bf16)
-    product = jnp.dot(stacked, returned, preferred_element_type=f32)
+    product = jnp.dot(
+        by_part(plan, part, (high, middle, low)), returned, preferred_element_type=f32
+    )
     t = plan.tokens
     pieces = []
     for p in range(plan.parts):
@@ -125,20 +105,28 @@
 
 
 def emit_dispatch(plan, state, gain, router, routes, slots_ref, weight_ref):
+    t = plan.tokens
+    first = column(routes[0:1], t)
+    second = column(routes[1:2], t)
+    part, expert, slot = plan.where(lax.broadcasted_iota(i32, (t, plan.total), 1))
+    is_first = first == expert
+    is_second = second == expert
+    named = jnp.where(is_first | is_second, 1.0, 0.0)
+    earlier = jnp.where(
+        lax.broadcasted_iota(i32, (t, t), 1) < lax.broadcasted_iota(i32, (t, t), 0), 1.0, 0.0
+    ).astype(bf16)
+    before = jnp.dot(earlier, named.astype(bf16), preferred_element_type=f32)
+    chosen = jnp.where(before == slot.astype(f32), named, 0.0)
+
     inverse = lax.rsqrt(jnp.mean(state * state, axis=1, keepdims=True) + epsilon)
     scaled = state * inverse * gain
     normed = scaled.astype(bf16)
-    first = routes[0:1]
-    second = routes[1:2]
-    select = dispatch_select(plan, first, second)
-    sent = jnp.zeros((plan.total, plan.piece), f32)
-    for p in range(plan.parts):
-        sent = sent + jnp.dot(
-            select[p],
-            normed[:, p * plan.piece : (p + 1) * plan.piece],
-            preferred_element_type=f32,
-        )
-    slots_ref[...] = sent.astype(bf16)
+    pieces = jnp.concatenate(
+        [normed[:, p * plan.piece : (p + 1) * plan.piece] for p in range(plan.parts)], axis=0
+    )
+    slots_ref[...] = lax.dot_general(
+        by_part(plan, part, (chosen,)), pieces, (((0,), (0,)), ((), ())), preferred_element_type=f32
+    ).astype(bf16)
     logits = lax.dot_general(
         scaled,
         router,
@@ -146,17 +134,14 @@
         precision=lax.Precision.HIGHEST,
         preferred_element_type=f32,
     )
-    first_column = column(first, plan.tokens)
-    second_column = column(second, plan.tokens)
-    lane = lax.broadcasted_iota(i32, (plan.tokens, plan.experts), 1)
+    lane = lax.broadcasted_iota(i32, (t, plan.experts), 1)
     gap = jnp.sum(
-        jnp.where(lane == first_column, logits, 0.0)
-        - jnp.where(lane == second_column, logits, 0.0),
+        jnp.where(lane == first, logits, 0.0) - jnp.where(lane == second, logits, 0.0),
         axis=1,
         keepdims=True,
     )
     mix = jax.nn.sigmoid(gap)
-    weight_ref[...] = combine_select(plan, first_column, second_column, mix)
+    weight_ref[...] = chosen * jnp.where(is_first, mix, 1.0 - mix)
 
 
 def per_device_fn(mesh):
@@ -275,31 +260,24 @@
 
         def compute(arrived, layer):
             def body(arrived_ref, up_ref, down_ref, out_ref):
-                base = lax.axis_index("mp") * mine if plan.share > 1 else 0
+                base = plan.first_expert({axis: lax.axis_index(axis) for axis in plan.shares})
                 total = plan.rows * plan.peers
 
-                def picks(shape, row_axis):
-                    row = lax.broadcasted_iota(i32, shape, row_axis)
-                    piece = lax.broadcasted_iota(i32, shape, 1 - row_axis)
-                    local = div(row, each)
-                    source = div(rem(row, each), CAP)
-                    target = source * plan.block + local * CAP + rem(row, CAP)
-                    return [
-                        jnp.where(piece == target + p * plan.rows, 1.0, 0.0).astype(bf16)
-                        for p in range(plan.parts)
-                    ]
-
-                arrived = arrived_ref[...]
+                def order(axis):
+                    shape = (plan.total, plan.total)
+                    row = lax.broadcasted_iota(i32, shape, axis)
+                    piece = lax.broadcasted_iota(i32, shape, 1 - axis)
+                    inner = rem(row, total)
+                    source = div(rem(inner, each), CAP)
+                    inside = div(row, total) * plan.rows + div(inner, each) * CAP + rem(row, CAP)
+                    return jnp.where(piece == source * plan.block + inside, 1.0, 0.0).astype(bf16)
+
+                ordered = jnp.dot(order(0), arrived_ref[...], preferred_element_type=f32).astype(bf16)
                 rows = jnp.concatenate(
-                    [
-                        jnp.dot(pick, arrived, preferred_element_type=f32).astype(bf16)
-                        for pick in picks((total, plan.total), 0)
-                    ],
-                    axis=1,
-                )
-                results = []
-                for local in range(mine):
-                    hid = jax.nn.gelu(
+                    [ordered[p * total : (p + 1) * total] for p in range(plan.parts)], axis=1
+                )
+                hids = [
+                    jax.nn.gelu(
                         lax.dot_general(
                             rows[local * each : (local + 1) * each],
                             up_ref[layer, base + local],
@@ -308,16 +286,21 @@
                         ),
                         approximate=True,
                     ).astype(bf16)
-                    results.append(
-                        jnp.dot(hid, down_ref[layer, base + local], preferred_element_type=f32).astype(bf16)
-                    )
-                result = jnp.concatenate(results, axis=0)
-                out = jnp.zeros((plan.total, plan.piece), f32)
-                for p, pick in enumerate(picks((plan.total, total), 1)):
-                    out = out + jnp.dot(
-                        pick, result[:, p * plan.piece : (p + 1) * plan.piece], preferred_element_type=f32
-                    )
-                out_ref[...] = out.astype(bf16)
+                    for local in range(mine)
+                ]
+                result = jnp.concatenate(
+                    [
+                        jnp.dot(hids[local], down_ref[layer, base + local], preferred_element_type=f32).astype(
+                            bf16
+                        )
+                        for local in range(mine)
+                    ],
+                    axis=0,
+                )
+                pieces = jnp.concatenate(
+                    [result[:, p * plan.piece : (p + 1) * plan.piece] for p in range(plan.parts)], axis=0
+                )
+                out_ref[...] = jnp.dot(order(1), pieces, preferred_element_type=f32).astype(bf16)
 
             return call(body, here(arrived, up_t, down_proj), [slots_shape], limit=6)[0]
 

time: 129 us -> 122 us (0.946)
  Pallas kernels: 20.7 us -> 14.3 us
    pallas_call x9, Pallas kernels: 20.7 us -> 14.3 us  [call(): pl.pallas_call(body, out_shape=outs, in_specs=[spec for spec, _ in args],...]
where the time goes in v4:
time: 122 us; the launch traced here: 121 us
  blocking collectives  106 us (87%)
  Pallas kernels  14.3 us (12%)
    all_to_all x8, blocking collectives, exchange(): return lax.all_to_all(x, plan.axes, split_axis=0, concat_axis=0, tiled=True)  106 us
    pallas_call x9, Pallas kernels, call(): pl.pallas_call(body, out_shape=outs, in_specs=[spec for spec, _ in args],...  14.3 us

profile of v4, /device:TPU:0, one launch (start us, length us, event | category | flops | bytes accessed | tf_op | source)
XLA Modules:
  0.0 121.2 jit_solution(8565915241368158130)
XLA Ops:
  0.6 0.0 copy-start
  0.6 0.0 copy-start.2
  0.7 2.0 %shard_map.86 = (f32[16,2048]{1,0:T(8,128)S(1)}, f32[1,2048]{1,0:T(1,128)S(1)}, f32[2,2048]{1,0:T(2,128)S(1)}, f32[2,16,2048]{2,1,0:T(8,128)S(1)}, s32[2,2,2,16]...) custom-call(f32[16,2048]{1,0:T(8,128)} %refs_0_.1, ...), custom_call_target="tpu_custom_call" | custom-call | flops 99999997952 | bytes 1000000000 | tf_op jit(solution)/shard_map/pallas_call | solution.py:152
  2.6 17.4 %all_to_all.88 = bf16[32,8,512]{2,1,0:T(8,128)(2,1)S(1)} all-to-all(bf16[32,8,512]{2,1,0:T(8,128)(2,1)S(1)} %bitcast.24), channel_id=1, replica_groups=mesh['groups'=2,'expert'=4,'dp'=2,'mp'=2] {'groups','expert','dp','mp'}, dimensions={0} | all-to-all | bytes 524288 | tf_op jit(solution)/shard_map/all_to_all | solution.py:308
  20.0 0.0 copy-done
  20.1 0.0 copy-done.2
  20.1 2.1 %shard_map.87 = bf16[256,512]{1,0:T(8,128)(2,1)S(1)} custom-call(bf16[256,512]{1,0:T(8,128)(2,1)S(1)} %bitcast.28, bf16[2,4,704,2048]{3,2,1,0:T(8,128)(2,1)S(1)} %bitcast.36, bf16[2,4,704,2048]{3,2,1,0:T(8,128)(2,1)S(1)} %copy-done.2), custom_call_target="tpu_custom_call" | custom-call | flops 99999997952 | bytes 1000000000 | tf_op jit(solution)/shard_map/pallas_call | solution.py:152
  22.2 12.6 %all_to_all.89 = bf16[32,8,512]{2,1,0:T(8,128)(2,1)S(1)} all-to-all(bf16[32,8,512]{2,1,0:T(8,128)(2,1)S(1)} %bitcast.29), channel_id=1, replica_groups=mesh['groups'=2,'expert'=4,'dp'=2,'mp'=2] {'groups','expert','dp','mp'}, dimensions={0} | all-to-all | bytes 524288 | tf_op jit(solution)/shard_map/all_to_all | solution.py:308
  34.8 0.0 copy-start.1
  34.8 0.0 copy-start.3
  34.8 0.9 shard_map.88
  35.8 12.6 %all_to_all.90 = bf16[32,8,512]{2,1,0:T(8,128)(2,1)S(1)} all-to-all(bf16[32,8,512]{2,1,0:T(8,128)(2,1)S(1)} %bitcast.27), channel_id=1, replica_groups=mesh['groups'=2,'expert'=4,'dp'=2,'mp'=2] {'groups','expert','dp','mp'}, dimensions={0} | all-to-all | bytes 524288 | tf_op jit(solution)/shard_map/all_to_all | solution.py:308
  48.4 0.0 copy-done.1
  48.4 0.5 copy-done.3
  48.9 2.1 %shard_map.89 = bf16[256,512]{1,0:T(8,128)(2,1)S(1)} custom-call(bf16[256,512]{1,0:T(8,128)(2,1)S(1)} %bitcast.30, bf16[2,4,704,2048]{3,2,1,0:T(8,128)(2,1)S(1)} %bitcast.37, bf16[2,4,704,2048]{3,2,1,0:T(8,128)(2,1)S(1)} %copy-done.3), custom_call_target="tpu_custom_call" | custom-call | flops 99999997952 | bytes 1000000000 | tf_op jit(solution)/shard_map/pallas_call | solution.py:152
  51.1 12.6 %all_to_all.91 = bf16[32,8,512]{2,1,0:T(8,128)(2,1)S(1)} all-to-all(bf16[32,8,512]{2,1,0:T(8,128)(2,1)S(1)} %bitcast.31), channel_id=1, replica_groups=mesh['groups'=2,'expert'=4,'dp'=2,'mp'=2] {'groups','expert','dp','mp'}, dimensions={0} | all-to-all | bytes 524288 | tf_op jit(solution)/shard_map/all_to_all | solution.py:308
  63.7 1.0 shard_map.90
  64.6 12.6 %all_to_all.92 = bf16[32,8,512]{2,1,0:T(8,128)(2,1)S(1)} all-to-all(bf16[32,8,512]{2,1,0:T(8,128)(2,1)S(1)} %bitcast.25), channel_id=1, replica_groups=mesh['groups'=2,'expert'=4,'dp'=2,'mp'=2] {'groups','expert','dp','mp'}, dimensions={0} | all-to-all | bytes 524288 | tf_op jit(solution)/shard_map/all_to_all | solution.py:308
  77.3 2.1 %shard_map.91 = bf16[256,512]{1,0:T(8,128)(2,1)S(1)} custom-call(bf16[256,512]{1,0:T(8,128)(2,1)S(1)} %bitcast.32, bf16[2,4,704,2048]{3,2,1,0:T(8,128)(2,1)S(1)} %bitcast.38, bf16[2,4,704,2048]{3,2,1,0:T(8,128)(2,1)S(1)} %copy-done.3), custom_call_target="tpu_custom_call" | custom-call | flops 99999997952 | bytes 1000000000 | tf_op jit(solution)/shard_map/pallas_call | solution.py:152
  79.4 12.6 %all_to_all.93 = bf16[32,8,512]{2,1,0:T(8,128)(2,1)S(1)} all-to-all(bf16[32,8,512]{2,1,0:T(8,128)(2,1)S(1)} %bitcast.33), channel_id=1, replica_groups=mesh['groups'=2,'expert'=4,'dp'=2,'mp'=2] {'groups','expert','dp','mp'}, dimensions={0} | all-to-all | bytes 524288 | tf_op jit(solution)/shard_map/all_to_all | solution.py:308
  92.0 0.9 shard_map.92
  93.0 12.6 %all_to_all.94 = bf16[32,8,512]{2,1,0:T(8,128)(2,1)S(1)} all-to-all(bf16[32,8,512]{2,1,0:T(8,128)(2,1)S(1)} %bitcast.22), channel_id=1, replica_groups=mesh['groups'=2,'expert'=4,'dp'=2,'mp'=2] {'groups','expert','dp','mp'}, dimensions={0} | all-to-all | bytes 524288 | tf_op jit(solution)/shard_map/all_to_all | solution.py:308
  105.6 2.1 %shard_map.93 = bf16[256,512]{1,0:T(8,128)(2,1)S(1)} custom-call(bf16[256,512]{1,0:T(8,128)(2,1)S(1)} %bitcast.34, bf16[2,4,704,2048]{3,2,1,0:T(8,128)(2,1)S(1)} %bitcast.39, bf16[2,4,704,2048]{3,2,1,0:T(8,128)(2,1)S(1)} %copy-done.3), custom_call_target="tpu_custom_call" | custom-call | flops 99999997952 | bytes 1000000000 | tf_op jit(solution)/shard_map/pallas_call | solution.py:152
  107.7 12.6 %all_to_all.95 = bf16[32,8,512]{2,1,0:T(8,128)(2,1)S(1)} all-to-all(bf16[32,8,512]{2,1,0:T(8,128)(2,1)S(1)} %bitcast.35), channel_id=1, replica_groups=mesh['groups'=2,'expert'=4,'dp'=2,'mp'=2] {'groups','expert','dp','mp'}, dimensions={0} | all-to-all | bytes 524288 | tf_op jit(solution)/shard_map/all_to_all | solution.py:308
  120.3 0.9 shard_map.94
Async XLA Ops:
  0.6 19.4 %copy-start = (bf16[2,4,2048,704]{2,3,1,0:T(8,128)(2,1)S(1)}, bf16[2,4,2048,704]{2,3,1,0:T(8,128)(2,1)}, u32[]{:S(2)}) copy-start(bf16[2,4,2048,704]{2,3,1,0:T(8,128)(2,1)} %param.11) | copy-start | bytes 69206016
  0.6 19.4 %copy-start.2 = (bf16[2,4,704,2048]{3,2,1,0:T(8,128)(2,1)S(1)}, bf16[2,4,704,2048]{3,2,1,0:T(8,128)(2,1)}, u32[]{:S(2)}) copy-start(bf16[2,4,704,2048]{3,2,1,0:T(8,128)(2,1)} %down_ref.7) | copy-start | bytes 69206016
  34.8 13.6 %copy-start.1 = (bf16[2,4,2048,704]{2,3,1,0:T(8,128)(2,1)S(1)}, bf16[2,4,2048,704]{2,3,1,0:T(8,128)(2,1)}, u32[]{:S(2)}) copy-start(bf16[2,4,2048,704]{2,3,1,0:T(8,128)(2,1)} %param.11) | copy-start | bytes 69206016
  34.8 14.1 %copy-start.3 = (bf16[2,4,704,2048]{3,2,1,0:T(8,128)(2,1)S(1)}, bf16[2,4,704,2048]{3,2,1,0:T(8,128)(2,1)}, u32[]{:S(2)}) copy-start(bf16[2,4,704,2048]{3,2,1,0:T(8,128)(2,1)} %down_ref.7) | copy-start | bytes 69206016

commit v5 on v4

--- a/solution.py
+++ b/solution.py
@@ -8,6 +8,7 @@
 from jax.sharding import PartitionSpec as P
 
 CAP = 2
+TERMS = 2
 
 epsilon = 1e-06
 start_time = 1.0
@@ -78,70 +79,83 @@
     return jnp.sum(jnp.where(eye, row, 0), axis=1, keepdims=True)
 
 
-def by_part(plan, part, terms):
-    return jnp.concatenate(
-        [jnp.where(part == p, term, 0.0) for p in range(plan.parts) for term in terms], axis=0
-    ).astype(bf16)
-
-
-def combine(plan, state, weight, returned):
-    part, _, _ = plan.where(lax.broadcasted_iota(i32, weight.shape, 1))
-    high = weight.astype(bf16).astype(f32)
-    middle = (weight - high).astype(bf16).astype(f32)
-    low = weight - high - middle
-    product = jnp.dot(
-        by_part(plan, part, (high, middle, low)), returned, preferred_element_type=f32
-    )
-    t = plan.tokens
-    pieces = []
-    for p in range(plan.parts):
-        base = 3 * t * p
-        pieces.append(
-            product[base : base + t]
-            + product[base + t : base + 2 * t]
-            + product[base + 2 * t : base + 3 * t]
-        )
-    return state + jnp.concatenate(pieces, axis=1)
-
-
-def emit_dispatch(plan, state, gain, router, routes, slots_ref, weight_ref):
+def split(x, terms):
+    out = []
+    for _ in range(terms):
+        out.append(x.astype(bf16))
+        x = x - out[-1].astype(f32)
+    return out
+
+
+def by_part(plan, part, term):
+    return [jnp.where(part == p, term, 0.0) for p in range(plan.parts)]
+
+
+def select(plan, routes):
     t = plan.tokens
     first = column(routes[0:1], t)
     second = column(routes[1:2], t)
     part, expert, slot = plan.where(lax.broadcasted_iota(i32, (t, plan.total), 1))
     is_first = first == expert
-    is_second = second == expert
-    named = jnp.where(is_first | is_second, 1.0, 0.0)
+    named = jnp.where(is_first | (second == expert), 1.0, 0.0)
     earlier = jnp.where(
         lax.broadcasted_iota(i32, (t, t), 1) < lax.broadcasted_iota(i32, (t, t), 0), 1.0, 0.0
     ).astype(bf16)
     before = jnp.dot(earlier, named.astype(bf16), preferred_element_type=f32)
     chosen = jnp.where(before == slot.astype(f32), named, 0.0)
-
-    inverse = lax.rsqrt(jnp.mean(state * state, axis=1, keepdims=True) + epsilon)
-    scaled = state * inverse * gain
-    normed = scaled.astype(bf16)
-    pieces = jnp.concatenate(
-        [normed[:, p * plan.piece : (p + 1) * plan.piece] for p in range(plan.parts)], axis=0
-    )
-    slots_ref[...] = lax.dot_general(
-        by_part(plan, part, (chosen,)), pieces, (((0,), (0,)), ((), ())), preferred_element_type=f32
-    ).astype(bf16)
-    logits = lax.dot_general(
-        scaled,
-        router,
+    return first, second, part, is_first, chosen
+
+
+def senders(plan, routes):
+    _, _, part, _, chosen = select(plan, routes)
+    return jnp.concatenate(by_part(plan, part, chosen), axis=0).T.astype(bf16)
+
+
+def weights_of(plan, scaled, router, routes):
+    first, second, part, is_first, chosen = select(plan, routes)
+    product = lax.dot_general(
+        jnp.concatenate(split(scaled, 3), axis=0),
+        jnp.concatenate(split(router, 3), axis=0),
         (((1,), (1,)), ((), ())),
-        precision=lax.Precision.HIGHEST,
         preferred_element_type=f32,
     )
-    lane = lax.broadcasted_iota(i32, (t, plan.experts), 1)
+    t = plan.tokens
+    logits = product[:t] + product[t : 2 * t] + product[2 * t :]
+    lane = rem(lax.broadcasted_iota(i32, logits.shape, 1), plan.experts)
     gap = jnp.sum(
         jnp.where(lane == first, logits, 0.0) - jnp.where(lane == second, logits, 0.0),
         axis=1,
         keepdims=True,
     )
     mix = jax.nn.sigmoid(gap)
-    weight_ref[...] = chosen * jnp.where(is_first, mix, 1.0 - mix)
+    weight = chosen * jnp.where(is_first, mix, 1.0 - mix)
+    return jnp.concatenate(
+        [term for piece in by_part(plan, part, weight) for term in split(piece, TERMS)], axis=0
+    )
+
+
+def combine(plan, state, weights, returned):
+    product = jnp.dot(weights, returned, preferred_element_type=f32)
+    t = plan.tokens
+    pieces = []
+    for p in range(plan.parts):
+        piece = product[TERMS * t * p : TERMS * t * p + t]
+        for term in range(1, TERMS):
+            base = t * (TERMS * p + term)
+            piece = piece + product[base : base + t]
+        pieces.append(piece)
+    return state + jnp.concatenate(pieces, axis=1)
+
+
+def emit_dispatch(plan, state, gain, gather, scaled_ref, slots_ref):
+    inverse = lax.rsqrt(jnp.mean(state * state, axis=1, keepdims=True) + epsilon)
+    scaled = state * inverse * gain
+    scaled_ref[...] = scaled
+    normed = scaled.astype(bf16)
+    pieces = jnp.concatenate(
+        [normed[:, p * plan.piece : (p + 1) * plan.piece] for p in range(plan.parts)], axis=0
+    )
+    slots_ref[...] = jnp.dot(gather, pieces, preferred_element_type=f32).astype(bf16)
 
 
 def per_device_fn(mesh):
@@ -181,85 +195,83 @@
         out_shape = jax.ShapeDtypeStruct((tokens, width), f32)
         state_shape = pltpu.VMEM((tokens, width), f32)
         slots_shape = pltpu.VMEM((plan.total, plan.piece), bf16)
-        weight_shape = pltpu.VMEM((tokens, plan.total), f32)
+        gather_shape = pltpu.VMEM((plan.total, plan.parts * tokens), bf16)
+        weight_shape = pltpu.VMEM((TERMS * plan.parts * tokens, plan.total), bf16)
+        sent = [state_shape, state_shape, slots_shape]
 
         def begin():
-            inputs = [latent, embedding, norm_gain, router_t, routes_t]
+            inputs = [latent, embedding, norm_gain, routes_t]
             count = len(inputs)
 
             def body(*refs):
                 sources, copies = refs[:count], refs[count : 2 * count]
-                state_ref, slots_ref, weight_ref, sems = refs[2 * count :]
+                state_ref, scaled_ref, slots_ref, sems = refs[2 * count :]
                 moves = [
                     pltpu.make_async_copy(source, target, sems.at[i])
                     for i, (source, target) in enumerate(zip(sources, copies))
                 ]
-                for move in moves:
+                for move in reversed(moves):
                     move.start()
-                for move in moves:
+                for move in reversed(moves):
                     move.wait()
-                latent_ref, emb_ref, gain_ref, router_ref, routes_ref = copies
+                latent_ref, emb_ref, gain_ref, routes_ref = copies
                 state = latent_ref[...] + start_time * emb_ref[...]
                 state_ref[...] = state
-                emit_dispatch(
-                    plan, state, gain_ref[0:1], router_ref[0], routes_ref[0, 0], slots_ref, weight_ref
-                )
+                gather = senders(plan, routes_ref[0, 0])
+                emit_dispatch(plan, state, gain_ref[0:1], gather, scaled_ref, slots_ref)
 
             outs = call(
                 body,
                 far(*inputs),
-                [pltpu.VMEM(x.shape, x.dtype) for x in inputs] + [state_shape, slots_shape, weight_shape],
+                [pltpu.VMEM(x.shape, x.dtype) for x in inputs] + sent,
                 copies=count,
             )
             return outs[:count], outs[count:]
 
-        def middle(small, step, layer, state, weight, returned):
-            def body(gain_ref, router_ref, routes_ref, state_in, weight_in, returned_ref,
-                     state_ref, slots_ref, weight_ref):
-                state = combine(plan, state_in[...], weight_in[...], returned_ref[...])
+        def middle(gain, layer, state, weights, gather, returned):
+            def body(gain_ref, state_in, weight_ref, gather_ref, returned_ref, state_ref, scaled_ref, slots_ref):
+                state = combine(plan, state_in[...], weight_ref[...], returned_ref[...])
                 state_ref[...] = state
                 emit_dispatch(
-                    plan, state, gain_ref[layer : layer + 1], router_ref[layer],
-                    routes_ref[step, layer], slots_ref, weight_ref,
+                    plan, state, gain_ref[layer : layer + 1], gather_ref[...], scaled_ref, slots_ref
                 )
 
-            return call(
-                body, here(*small[2:], state, weight, returned), [state_shape, slots_shape, weight_shape]
-            )
-
-        def turn(small, state, weight, returned):
-            def body(latent_ref, emb_ref, gain_ref, router_ref, routes_ref, state_in, weight_in, returned_ref,
-                     first_ref, state_ref, slots_ref, weight_ref):
-                state = combine(plan, state_in[...], weight_in[...], returned_ref[...])
+            return call(body, here(gain, state, weights, gather, returned), sent)
+
+        def turn(latent_s, emb, gain, state, weights, gather, returned):
+            def body(latent_ref, emb_ref, gain_ref, state_in, weight_ref, gather_ref, returned_ref,
+                     first_ref, state_ref, scaled_ref, slots_ref):
+                state = combine(plan, state_in[...], weight_ref[...], returned_ref[...])
                 first = state - latent_ref[...]
                 first_ref[...] = first
                 moved = latent_ref[...] + step_size * first
                 state = moved + (start_time + step_size) * emb_ref[...]
                 state_ref[...] = state
-                emit_dispatch(
-                    plan, state, gain_ref[0:1], router_ref[0], routes_ref[1, 0], slots_ref, weight_ref
-                )
+                emit_dispatch(plan, state, gain_ref[0:1], gather_ref[...], scaled_ref, slots_ref)
 
             return call(
-                body, here(*small, state, weight, returned),
-                [state_shape, state_shape, slots_shape, weight_shape],
+                body, here(latent_s, emb, gain, state, weights, gather, returned), [state_shape] + sent
             )
 
-        def finish(small, state, weight, returned, first):
-            def body(latent_ref, state_in, weight_in, returned_ref, first_ref, next_ref, mean_ref):
-                state = combine(plan, state_in[...], weight_in[...], returned_ref[...])
+        def finish(latent_s, state, weights, returned, first):
+            def body(latent_ref, state_in, weight_ref, returned_ref, first_ref, next_ref, mean_ref):
+                state = combine(plan, state_in[...], weight_ref[...], returned_ref[...])
                 first = first_ref[...]
                 moved = latent_ref[...] + step_size * first
                 mean = 0.5 * (first + (state - moved))
                 mean_ref[...] = mean
                 next_ref[...] = latent_ref[...] + step_size * mean
 
-            return call(body, here(small[0], state, weight, returned, first), [out_shape, out_shape])
+            return call(body, here(latent_s, state, weights, returned, first), [out_shape, out_shape])
 
         each = plan.peers * CAP
 
-        def compute(arrived, layer):
-            def body(arrived_ref, up_ref, down_ref, out_ref):
+        def compute(arrived, scaled, routes_s, step, layer):
+            follows = step * layers + layer + 1
+            last = follows == 2 * layers
+
+            def body(arrived_ref, up_ref, down_ref, scaled_ref, router_ref, routes_ref,
+                     out_ref, weight_ref, *gather_ref):
                 base = plan.first_expert({axis: lax.axis_index(axis) for axis in plan.shares})
                 total = plan.rows * plan.peers
 
@@ -288,6 +300,9 @@
                     ).astype(bf16)
                     for local in range(mine)
                 ]
+                weight_ref[...] = weights_of(plan, scaled_ref[...], router_ref[layer], routes_ref[step, layer])
+                if not last:
+                    gather_ref[0][...] = senders(plan, routes_ref[follows // layers, follows % layers])
                 result = jnp.concatenate(
                     [
                         jnp.dot(hids[local], down_ref[layer, base + local], preferred_element_type=f32).astype(
@@ -302,21 +317,29 @@
                 )
                 out_ref[...] = jnp.dot(order(1), pieces, preferred_element_type=f32).astype(bf16)
 
-            return call(body, here(arrived, up_t, down_proj), [slots_shape], limit=6)[0]
+            return call(
+                body,
+                here(arrived, up_t, down_proj, scaled, router_t, routes_s),
+                [slots_shape, weight_shape] + [gather_shape] * (not last),
+                limit=6,
+            )
 
         def exchange(x):
             return lax.all_to_all(x, plan.axes, split_axis=0, concat_axis=0, tiled=True)
 
-        small, (state, slots, weight) = begin()
+        (latent_s, emb, gain, routes_s), (state, scaled, slots) = begin()
         for step in range(2):
             for layer in range(layers):
-                returned = exchange(compute(exchange(slots), layer))
+                result, weights, *gather = compute(exchange(slots), scaled, routes_s, step, layer)
+                returned = exchange(result)
                 if layer + 1 < layers:
-                    state, slots, weight = middle(small, step, layer + 1, state, weight, returned)
+                    state, scaled, slots = middle(gain, layer + 1, state, weights, *gather, returned)
                 elif step == 0:
-                    first, state, slots, weight = turn(small, state, weight, returned)
+                    first, state, scaled, slots = turn(
+                        latent_s, emb, gain, state, weights, *gather, returned
+                    )
                 else:
-                    return tuple(finish(small, state, weight, returned, first))
+                    return tuple(finish(latent_s, state, weights, returned, first))
 
     return run
 

time: 122 us -> 120 us (0.984)
  Pallas kernels: 14.3 us -> 12.6 us
    pallas_call x9, Pallas kernels: 14.3 us -> 12.6 us  [call(): pl.pallas_call(body, out_shape=outs, in_specs=[spec for spec, _ in args],...]
where the time goes in v5:
time: 120 us
  blocking collectives  106 us (88%)
  Pallas kernels  12.6 us (10%)
    all_to_all x8, blocking collectives, exchange(): return lax.all_to_all(x, plan.axes, split_axis=0, concat_axis=0, tiled=True)  106 us
    pallas_call x9, Pallas kernels, call(): pl.pallas_call(body, out_shape=outs, in_specs=[spec for spec, _ in args],...  12.6 us

profile of v5, /device:TPU:0, one launch (start us, length us, event | category | flops | bytes accessed | tf_op | source)
XLA Modules:
  0.0 120.0 jit_solution(2552144353463264978)
XLA Ops:
  0.6 0.0 copy-start
  0.6 0.0 copy-start.2
  0.7 0.0 copy-start.4
  0.7 1.6 %shard_map.86 = (f32[16,2048]{1,0:T(8,128)S(1)}, f32[1,2048]{1,0:T(1,128)S(1)}, f32[2,2048]{1,0:T(2,128)S(1)}, s32[2,2,2,16]{3,2,1,0:T(2,128)S(1)}, f32[16,2048]...) custom-call(f32[16,2048]{1,0:T(8,128)} %refs_0_.1, f32[1,2048]{1,0:T(1,128)} %bitcast.44, ...), custom_call_target="tpu_custom_call" | custom-call | flops 99999997952 | bytes 1000000000 | tf_op jit(solution)/shard_map/pallas_call | solution.py:166
  2.3 17.4 %all_to_all.88 = bf16[32,8,512]{2,1,0:T(8,128)(2,1)S(1)} all-to-all(bf16[32,8,512]{2,1,0:T(8,128)(2,1)S(1)} %bitcast.26), channel_id=1, replica_groups=mesh['groups'=2,'expert'=4,'dp'=2,'mp'=2] {'groups','expert','dp','mp'}, dimensions={0} | all-to-all | bytes 524288 | tf_op jit(solution)/shard_map/all_to_all | solution.py:328
  19.7 0.0 copy-done
  19.7 0.0 copy-done.2
  19.7 0.0 copy-done.4
  19.7 2.2 %shard_map.87 = (bf16[256,512]{1,0:T(8,128)(2,1)S(1)}, bf16[128,256]{1,0:T(8,128)(2,1)S(1)}, bf16[256,64]{1,0:T(8,128)(2,1)S(1)}) custom-call(bf16[256,512]{1,0:T(8,128)(2,1)S(1)} %bitcast.28, bf16[2,4,704,2048]{3,2,1,0:T(8,128)(2,1)S(1)} %bitcast.36, bf16[2,4,704,2048]{3,2,1,0:T(8,128)(2,1)S(1)} %copy-done.2, f32[16,2048]{1,0:T(8,128)S(1)} %get-tuple-element.35.scaled_ref, ...), custom_call_target="tpu_custom_call" | custom-call | flops 99999997952 | bytes 1000000000 | tf_op jit(solution)/shard_map/pallas_call | solution.py:166
  21.9 12.6 %all_to_all.89 = bf16[32,8,512]{2,1,0:T(8,128)(2,1)S(1)} all-to-all(bf16[32,8,512]{2,1,0:T(8,128)(2,1)S(1)} %bitcast.29), channel_id=1, replica_groups=mesh['groups'=2,'expert'=4,'dp'=2,'mp'=2] {'groups','expert','dp','mp'}, dimensions={0} | all-to-all | bytes 524288 | tf_op jit(solution)/shard_map/all_to_all | solution.py:328
  34.5 0.0 copy-start.1
  34.5 0.0 copy-start.3
  34.5 0.5 shard_map.88
  35.0 12.6 %all_to_all.90 = bf16[32,8,512]{2,1,0:T(8,128)(2,1)S(1)} all-to-all(bf16[32,8,512]{2,1,0:T(8,128)(2,1)S(1)} %bitcast.27), channel_id=1, replica_groups=mesh['groups'=2,'expert'=4,'dp'=2,'mp'=2] {'groups','expert','dp','mp'}, dimensions={0} | all-to-all | bytes 524288 | tf_op jit(solution)/shard_map/all_to_all | solution.py:328
  47.6 0.0 copy-done.1
  47.6 1.0 copy-done.3
  48.6 2.2 %shard_map.89 = (bf16[256,512]{1,0:T(8,128)(2,1)S(1)}, bf16[128,256]{1,0:T(8,128)(2,1)S(1)}, bf16[256,64]{1,0:T(8,128)(2,1)S(1)}) custom-call(bf16[256,512]{1,0:T(8,128)(2,1)S(1)} %bitcast.30, bf16[2,4,704,2048]{3,2,1,0:T(8,128)(2,1)S(1)} %bitcast.37, bf16[2,4,704,2048]{3,2,1,0:T(8,128)(2,1)S(1)} %copy-done.3, f32[16,2048]{1,0:T(8,128)S(1)} %get-tuple-element.42.scaled_ref, ...), custom_call_target="tpu_custom_call" | custom-call | flops 99999997952 | bytes 1000000000 | tf_op jit(solution)/shard_map/pallas_call | solution.py:166
  50.7 12.6 %all_to_all.91 = bf16[32,8,512]{2,1,0:T(8,128)(2,1)S(1)} all-to-all(bf16[32,8,512]{2,1,0:T(8,128)(2,1)S(1)} %bitcast.31), channel_id=1, replica_groups=mesh['groups'=2,'expert'=4,'dp'=2,'mp'=2] {'groups','expert','dp','mp'}, dimensions={0} | all-to-all | bytes 524288 | tf_op jit(solution)/shard_map/all_to_all | solution.py:328
  63.3 0.5 shard_map.90
  63.8 12.6 %all_to_all.92 = bf16[32,8,512]{2,1,0:T(8,128)(2,1)S(1)} all-to-all(bf16[32,8,512]{2,1,0:T(8,128)(2,1)S(1)} %bitcast.22), channel_id=1, replica_groups=mesh['groups'=2,'expert'=4,'dp'=2,'mp'=2] {'groups','expert','dp','mp'}, dimensions={0} | all-to-all | bytes 524288 | tf_op jit(solution)/shard_map/all_to_all | solution.py:328
  76.4 2.2 %shard_map.91 = (bf16[256,512]{1,0:T(8,128)(2,1)S(1)}, bf16[128,256]{1,0:T(8,128)(2,1)S(1)}, bf16[256,64]{1,0:T(8,128)(2,1)S(1)}) custom-call(bf16[256,512]{1,0:T(8,128)(2,1)S(1)} %bitcast.32, bf16[2,4,704,2048]{3,2,1,0:T(8,128)(2,1)S(1)} %bitcast.38, bf16[2,4,704,2048]{3,2,1,0:T(8,128)(2,1)S(1)} %copy-done.3, f32[16,2048]{1,0:T(8,128)S(1)} %get-tuple-element.48.scaled_ref, ...), custom_call_target="tpu_custom_call" | custom-call | flops 99999997952 | bytes 1000000000 | tf_op jit(solution)/shard_map/pallas_call | solution.py:166
  78.6 12.6 %all_to_all.93 = bf16[32,8,512]{2,1,0:T(8,128)(2,1)S(1)} all-to-all(bf16[32,8,512]{2,1,0:T(8,128)(2,1)S(1)} %bitcast.33), channel_id=1, replica_groups=mesh['groups'=2,'expert'=4,'dp'=2,'mp'=2] {'groups','expert','dp','mp'}, dimensions={0} | all-to-all | bytes 524288 | tf_op jit(solution)/shard_map/all_to_all | solution.py:328
  91.2 0.5 shard_map.92
  91.7 12.6 %all_to_all.94 = bf16[32,8,512]{2,1,0:T(8,128)(2,1)S(1)} all-to-all(bf16[32,8,512]{2,1,0:T(8,128)(2,1)S(1)} %bitcast.25), channel_id=1, replica_groups=mesh['groups'=2,'expert'=4,'dp'=2,'mp'=2] {'groups','expert','dp','mp'}, dimensions={0} | all-to-all | bytes 524288 | tf_op jit(solution)/shard_map/all_to_all | solution.py:328
  104.3 2.2 %shard_map.93 = (bf16[256,512]{1,0:T(8,128)(2,1)S(1)}, bf16[128,256]{1,0:T(8,128)(2,1)S(1)}) custom-call(bf16[256,512]{1,0:T(8,128)(2,1)S(1)} %bitcast.34, bf16[2,4,704,2048]{3,2,1,0:T(8,128)(2,1)S(1)} %bitcast.39, bf16[2,4,704,2048]{3,2,1,0:T(8,128)(2,1)S(1)} %copy-done.3, f32[16,2048]{1,0:T(8,128)S(1)} %get-tuple-element.54.scaled_ref, ...), custom_call_target="tpu_custom_call" | custom-call | flops 99999997952 | bytes 1000000000 | tf_op jit(solution)/shard_map/pallas_call | solution.py:166
  106.5 12.6 %all_to_all.95 = bf16[32,8,512]{2,1,0:T(8,128)(2,1)S(1)} all-to-all(bf16[32,8,512]{2,1,0:T(8,128)(2,1)S(1)} %bitcast.35), channel_id=1, replica_groups=mesh['groups'=2,'expert'=4,'dp'=2,'mp'=2] {'groups','expert','dp','mp'}, dimensions={0} | all-to-all | bytes 524288 | tf_op jit(solution)/shard_map/all_to_all | solution.py:328
  119.1 0.9 shard_map.94
Async XLA Ops:
  0.6 19.1 %copy-start = (bf16[2,4,2048,704]{2,3,1,0:T(8,128)(2,1)S(1)}, bf16[2,4,2048,704]{2,3,1,0:T(8,128)(2,1)}, u32[]{:S(2)}) copy-start(bf16[2,4,2048,704]{2,3,1,0:T(8,128)(2,1)} %param.11) | copy-start | bytes 69206016
  0.6 19.1 %copy-start.2 = (bf16[2,4,704,2048]{3,2,1,0:T(8,128)(2,1)S(1)}, bf16[2,4,704,2048]{3,2,1,0:T(8,128)(2,1)}, u32[]{:S(2)}) copy-start(bf16[2,4,704,2048]{3,2,1,0:T(8,128)(2,1)} %down_ref.7) | copy-start | bytes 69206016
  0.7 19.0 %copy-start.4 = (f32[2,2048,16]{1,2,0:T(8,128)S(1)}, f32[2,2048,16]{1,2,0:T(8,128)}, u32[]{:S(2)}) copy-start(f32[2,2048,16]{1,2,0:T(8,128)} %param.10) | copy-start | bytes 786436
  34.5 13.1 %copy-start.1 = (bf16[2,4,2048,704]{2,3,1,0:T(8,128)(2,1)S(1)}, bf16[2,4,2048,704]{2,3,1,0:T(8,128)(2,1)}, u32[]{:S(2)}) copy-start(bf16[2,4,2048,704]{2,3,1,0:T(8,128)(2,1)} %param.11) | copy-start | bytes 69206016
  34.5 14.1 %copy-start.3 = (bf16[2,4,704,2048]{3,2,1,0:T(8,128)(2,1)S(1)}, bf16[2,4,704,2048]{3,2,1,0:T(8,128)(2,1)}, u32[]{:S(2)}) copy-start(bf16[2,4,704,2048]{3,2,1,0:T(8,128)(2,1)} %down_ref.7) | copy-start | bytes 69206016

commit v6 on v5

--- a/solution.py
+++ b/solution.py
@@ -162,7 +162,7 @@
     vmem = pl.BlockSpec(memory_space=pltpu.VMEM)
     hbm = pl.BlockSpec(memory_space=pltpu.HBM)
 
-    def call(body, args, outs, copies=0, limit=4):
+    def call(body, args, outs, copies=0, limit=4, cost=10**11):
         return pl.pallas_call(
             body,
             out_shape=outs,
@@ -170,7 +170,7 @@
             out_specs=[vmem] * len(outs),
             scratch_shapes=[pltpu.SemaphoreType.DMA((copies,))] if copies else [],
             compiler_params=pltpu.CompilerParams(vmem_limit_bytes=limit << 20),
-            cost_estimate=pl.CostEstimate(flops=10**11, transcendentals=0, bytes_accessed=10**9),
+            cost_estimate=pl.CostEstimate(flops=cost, transcendentals=0, bytes_accessed=0),
         )(*[arg for _, arg in args])
 
     def here(*arrays):
@@ -236,7 +236,7 @@
                     plan, state, gain_ref[layer : layer + 1], gather_ref[...], scaled_ref, slots_ref
                 )
 
-            return call(body, here(gain, state, weights, gather, returned), sent)
+            return call(body, here(gain, state, weights, gather, returned), sent, cost=12300000000)
 
         def turn(latent_s, emb, gain, state, weights, gather, returned):
             def body(latent_ref, emb_ref, gain_ref, state_in, weight_ref, gather_ref, returned_ref,
@@ -288,18 +288,17 @@
                 rows = jnp.concatenate(
                     [ordered[p * total : (p + 1) * total] for p in range(plan.parts)], axis=1
                 )
-                hids = [
-                    jax.nn.gelu(
-                        lax.dot_general(
-                            rows[local * each : (local + 1) * each],
-                            up_ref[layer, base + local],
-                            (((1,), (1,)), ((), ())),
-                            preferred_element_type=f32,
-                        ),
-                        approximate=True,
-                    ).astype(bf16)
-                    for local in range(mine)
-                ]
+                hids = []
+                for local in range(mine):
+                    cuts = [0, -(-hidden // 256) * 128, hidden]
+                    hids.append(jnp.concatenate([
+                        jax.nn.gelu(
+                            lax.dot_general(
+                                rows[local * each : (local + 1) * each],
+                                up_ref[layer, base + local, lo:hi],
+                                (((1,), (1,)), ((), ())), preferred_element_type=f32,
+                            ), approximate=True).astype(bf16)
+                        for lo, hi in zip(cuts, cuts[1:])], axis=1))
                 weight_ref[...] = weights_of(plan, scaled_ref[...], router_ref[layer], routes_ref[step, layer])
                 if not last:
                     gather_ref[0][...] = senders(plan, routes_ref[follows // layers, follows % layers])

time: 120 us -> 118 us (0.983)
  no operation moved by 1% of the time
where the time goes in v6:
time: 118 us
  blocking collectives  106 us (90%)
  Pallas kernels  11.6 us (10%)
    all_to_all x8, blocking collectives, exchange(): return lax.all_to_all(x, plan.axes, split_axis=0, concat_axis=0, tiled=True)  106 us
    pallas_call x9, Pallas kernels, call(): pl.pallas_call(body, out_shape=outs, in_specs=[spec for spec, _ in args],...  11.6 us

profile of v6, /device:TPU:0, one launch (start us, length us, event | category | flops | bytes accessed | tf_op | source)
XLA Modules:
  0.0 118.1 jit_solution(13891829965080547597)
XLA Ops:
  0.6 0.0 copy-start
  0.6 0.0 copy-start.1
  0.7 0.0 copy-start.3
  0.7 1.6 %shard_map.86 = (f32[16,2048]{1,0:T(8,128)S(1)}, f32[1,2048]{1,0:T(1,128)S(1)}, f32[2,2048]{1,0:T(2,128)S(1)}, s32[2,2,2,16]{3,2,1,0:T(2,128)S(1)}, f32[16,2048]...) custom-call(f32[16,2048]{1,0:T(8,128)} %refs_0_.1, f32[1,2048]{1,0:T(1,128)} %bitcast.46, ...), custom_call_target="tpu_custom_call" | custom-call | flops 99999997952 | tf_op jit(solution)/shard_map/pallas_call | solution.py:166
  2.3 17.4 %all_to_all.88 = bf16[32,8,512]{2,1,0:T(8,128)(2,1)S(1)} all-to-all(bf16[32,8,512]{2,1,0:T(8,128)(2,1)S(1)} %bitcast.26), channel_id=1, replica_groups=mesh['groups'=2,'expert'=4,'dp'=2,'mp'=2] {'groups','expert','dp','mp'}, dimensions={0} | all-to-all | bytes 524288 | tf_op jit(solution)/shard_map/all_to_all | solution.py:327
  19.7 0.0 copy-done
  19.7 0.0 copy-done.1
  19.7 0.0 copy-done.3
  19.7 1.9 %shard_map.87 = (bf16[256,512]{1,0:T(8,128)(2,1)S(1)}, bf16[128,256]{1,0:T(8,128)(2,1)S(1)}, bf16[256,64]{1,0:T(8,128)(2,1)S(1)}) custom-call(bf16[256,512]{1,0:T(8,128)(2,1)S(1)} %bitcast.28, bf16[2,4,704,2048]{3,2,1,0:T(8,128)(2,1)S(1)} %bitcast.36, bf16[2,4,704,2048]{3,2,1,0:T(8,128)(2,1)S(1)} %copy-done.1, f32[16,2048]{1,0:T(8,128)S(1)} %get-tuple-element.35.scaled_ref, ...), custom_call_target="tpu_custom_call" | custom-call | flops 99999997952 | tf_op jit(solution)/shard_map/pallas_call | solution.py:166
  21.6 0.0 copy-start.2
  21.7 12.6 %all_to_all.89 = bf16[32,8,512]{2,1,0:T(8,128)(2,1)S(1)} all-to-all(bf16[32,8,512]{2,1,0:T(8,128)(2,1)S(1)} %bitcast.29), channel_id=1, replica_groups=mesh['groups'=2,'expert'=4,'dp'=2,'mp'=2] {'groups','expert','dp','mp'}, dimensions={0} | all-to-all | bytes 524288 | tf_op jit(solution)/shard_map/all_to_all | solution.py:327
  34.3 0.0 slice-start.4
  34.3 0.0 slice-start.5
  34.3 0.5 shard_map.88
  34.8 12.6 %all_to_all.90 = bf16[32,8,512]{2,1,0:T(8,128)(2,1)S(1)} all-to-all(bf16[32,8,512]{2,1,0:T(8,128)(2,1)S(1)} %bitcast.27), channel_id=1, replica_groups=mesh['groups'=2,'expert'=4,'dp'=2,'mp'=2] {'groups','expert','dp','mp'}, dimensions={0} | all-to-all | bytes 524288 | tf_op jit(solution)/shard_map/all_to_all | solution.py:327
  47.4 0.0 copy-done.2
  47.4 0.0 slice-done
  47.4 0.0 slice-done.1
  47.4 0.0 slice-done.2
  47.4 0.0 slice-done.3
  47.4 0.0 slice-done.4
  47.4 1.9 %shard_map.89 = (bf16[256,512]{1,0:T(8,128)(2,1)S(1)}, bf16[128,256]{1,0:T(8,128)(2,1)S(1)}, bf16[256,64]{1,0:T(8,128)(2,1)S(1)}) custom-call(bf16[256,512]{1,0:T(8,128)(2,1)S(1)} %bitcast.30, bf16[2,4,704,2048]{3,2,1,0:T(8,128)(2,1)S(1)} %bitcast.39, bf16[2,4,704,2048]{3,2,1,0:T(8,128)(2,1)S(1)} %copy-done.2, f32[16,2048]{1,0:T(8,128)S(1)} %get-tuple-element.42.scaled_ref, ...), custom_call_target="tpu_custom_call" | custom-call | flops 99999997952 | tf_op jit(solution)/shard_map/pallas_call | solution.py:166
  49.4 12.6 %all_to_all.91 = bf16[32,8,512]{2,1,0:T(8,128)(2,1)S(1)} all-to-all(bf16[32,8,512]{2,1,0:T(8,128)(2,1)S(1)} %bitcast.31), channel_id=1, replica_groups=mesh['groups'=2,'expert'=4,'dp'=2,'mp'=2] {'groups','expert','dp','mp'}, dimensions={0} | all-to-all | bytes 524288 | tf_op jit(solution)/shard_map/all_to_all | solution.py:327
  62.0 0.5 shard_map.90
  62.5 12.6 %all_to_all.92 = bf16[32,8,512]{2,1,0:T(8,128)(2,1)S(1)} all-to-all(bf16[32,8,512]{2,1,0:T(8,128)(2,1)S(1)} %bitcast.22), channel_id=1, replica_groups=mesh['groups'=2,'expert'=4,'dp'=2,'mp'=2] {'groups','expert','dp','mp'}, dimensions={0} | all-to-all | bytes 524288 | tf_op jit(solution)/shard_map/all_to_all | solution.py:327
  75.1 1.9 %shard_map.91 = (bf16[256,512]{1,0:T(8,128)(2,1)S(1)}, bf16[128,256]{1,0:T(8,128)(2,1)S(1)}, bf16[256,64]{1,0:T(8,128)(2,1)S(1)}) custom-call(bf16[256,512]{1,0:T(8,128)(2,1)S(1)} %bitcast.32, bf16[2,4,704,2048]{3,2,1,0:T(8,128)(2,1)S(1)} %bitcast.40, bf16[2,4,704,2048]{3,2,1,0:T(8,128)(2,1)S(1)} %copy-done.2, f32[16,2048]{1,0:T(8,128)S(1)} %get-tuple-element.48.scaled_ref, ...), custom_call_target="tpu_custom_call" | custom-call | flops 99999997952 | tf_op jit(solution)/shard_map/pallas_call | solution.py:166
  77.0 12.6 %all_to_all.93 = bf16[32,8,512]{2,1,0:T(8,128)(2,1)S(1)} all-to-all(bf16[32,8,512]{2,1,0:T(8,128)(2,1)S(1)} %bitcast.33), channel_id=1, replica_groups=mesh['groups'=2,'expert'=4,'dp'=2,'mp'=2] {'groups','expert','dp','mp'}, dimensions={0} | all-to-all | bytes 524288 | tf_op jit(solution)/shard_map/all_to_all | solution.py:327
  89.6 0.5 shard_map.92
  90.1 12.6 %all_to_all.94 = bf16[32,8,512]{2,1,0:T(8,128)(2,1)S(1)} all-to-all(bf16[32,8,512]{2,1,0:T(8,128)(2,1)S(1)} %bitcast.25), channel_id=1, replica_groups=mesh['groups'=2,'expert'=4,'dp'=2,'mp'=2] {'groups','expert','dp','mp'}, dimensions={0} | all-to-all | bytes 524288 | tf_op jit(solution)/shard_map/all_to_all | solution.py:327
  102.7 1.8 %shard_map.93 = (bf16[256,512]{1,0:T(8,128)(2,1)S(1)}, bf16[128,256]{1,0:T(8,128)(2,1)S(1)}) custom-call(bf16[256,512]{1,0:T(8,128)(2,1)S(1)} %bitcast.34, bf16[2,4,704,2048]{3,2,1,0:T(8,128)(2,1)S(1)} %bitcast.41, bf16[2,4,704,2048]{3,2,1,0:T(8,128)(2,1)S(1)} %copy-done.2, f32[16,2048]{1,0:T(8,128)S(1)} %get-tuple-element.54.scaled_ref, ...), custom_call_target="tpu_custom_call" | custom-call | flops 99999997952 | tf_op jit(solution)/shard_map/pallas_call | solution.py:166
  104.6 12.6 %all_to_all.95 = bf16[32,8,512]{2,1,0:T(8,128)(2,1)S(1)} all-to-all(bf16[32,8,512]{2,1,0:T(8,128)(2,1)S(1)} %bitcast.35), channel_id=1, replica_groups=mesh['groups'=2,'expert'=4,'dp'=2,'mp'=2] {'groups','expert','dp','mp'}, dimensions={0} | all-to-all | bytes 524288 | tf_op jit(solution)/shard_map/all_to_all | solution.py:327
  117.2 0.9 shard_map.94
  (6 shorter events, 0.0 us)
Async XLA Ops:
  0.6 19.1 %copy-start = (bf16[2,4,2048,704]{2,3,1,0:T(8,128)(2,1)S(1)}, bf16[2,4,2048,704]{2,3,1,0:T(8,128)(2,1)}, u32[]{:S(2)}) copy-start(bf16[2,4,2048,704]{2,3,1,0:T(8,128)(2,1)} %param.11) | copy-start | bytes 69206016
  0.6 19.1 %copy-start.1 = (bf16[2,4,704,2048]{3,2,1,0:T(8,128)(2,1)S(1)}, bf16[2,4,704,2048]{3,2,1,0:T(8,128)(2,1)}, u32[]{:S(2)}) copy-start(bf16[2,4,704,2048]{3,2,1,0:T(8,128)(2,1)} %down_ref.7) | copy-start | bytes 69206016
  0.7 19.0 %copy-start.3 = (f32[2,2048,16]{1,2,0:T(8,128)S(1)}, f32[2,2048,16]{1,2,0:T(8,128)}, u32[]{:S(2)}) copy-start(f32[2,2048,16]{1,2,0:T(8,128)} %param.10) | copy-start | bytes 786436
  21.6 25.7 %copy-start.2 = (bf16[2,4,704,2048]{3,2,1,0:T(8,128)(2,1)S(1)}, bf16[2,4,704,2048]{3,2,1,0:T(8,128)(2,1)}, u32[]{:S(2)}) copy-start(bf16[2,4,704,2048]{3,2,1,0:T(8,128)(2,1)} %down_ref.7) | copy-start | bytes 69206016
  34.3 13.1 %slice-start = ((s8[23068672]{0:T(1024)(128)(4,1)}), s8[4194304]{0:T(1024)(128)(4,1)S(1)}, s32[]{:S(2)}) async-start(s8[23068672]{0:T(1024)(128)(4,1)} %bitcast.37), calls=%async_computation.8 | async-start | bytes 8388608
  34.3 13.1 %slice-start.1 = ((s8[23068672]{0:T(1024)(128)(4,1)}), s8[4194304]{0:T(1024)(128)(4,1)S(1)}, s32[]{:S(2)}) async-start(s8[23068672]{0:T(1024)(128)(4,1)} %bitcast.37), calls=%async_computation.9 | async-start | bytes 8388608
  34.3 13.1 %slice-start.2 = ((s8[23068672]{0:T(1024)(128)(4,1)}), s8[4194304]{0:T(1024)(128)(4,1)S(1)}, s32[]{:S(2)}) async-start(s8[23068672]{0:T(1024)(128)(4,1)} %bitcast.37), calls=%async_computation.10 | async-start | bytes 8388608
  34.3 13.1 %slice-start.3 = ((s8[23068672]{0:T(1024)(128)(4,1)}), s8[4194304]{0:T(1024)(128)(4,1)S(1)}, s32[]{:S(2)}) async-start(s8[23068672]{0:T(1024)(128)(4,1)} %bitcast.37), calls=%async_computation.11 | async-start | bytes 8388608
  34.3 13.1 %slice-start.4 = ((s8[23068672]{0:T(1024)(128)(4,1)}), s8[4194304]{0:T(1024)(128)(4,1)S(1)}, s32[]{:S(2)}) async-start(s8[23068672]{0:T(1024)(128)(4,1)} %bitcast.37), calls=%async_computation.12 | async-start | bytes 8388608
  34.3 13.1 %slice-start.5 = ((s8[23068672]{0:T(1024)(128)(4,1)}), s8[2097152]{0:T(1024)(128)(4,1)S(1)}, s32[]{:S(2)}) async-start(s8[23068672]{0:T(1024)(128)(4,1)} %bitcast.37), calls=%async_computation.13 | async-start | bytes 4194304
